TPU v7x, 256 devices: a whole 4x4x8 slice. The times are simulated.
256 devices in a mesh: frame: 8 (over z_hi, core), fsdp: 32 (over x, z_lo, y).
Axes of the slice: x: 4, y: 4, z: 8 (z_hi: 4, z_lo: 2; z = z_hi * 2 + z_lo), core: 2. Of those that a mesh axis runs over, the one named last changes fastest.
Arguments:
- window: bfloat16 [8, 512, 5120], P('frame', 'fsdp'), may hold values from -6 to 6
- levels: int32 [8], P('frame'), may hold values from 0 to 15
- actions: int32 [8], P('frame'), may hold values from 0 to 15
- cache_len: int32 [1], replicated, may hold values from 512 to 15872
- level_table: float32 [16, 3, 5120], replicated, may hold values from -4 to 4
- action_table: float32 [16, 3, 5120], replicated, may hold values from -4 to 4
- w_qkv: bfloat16 [3, 5120, 4096], P(None, None, 'fsdp'), may hold values from -0.078125 to 0.078125
- w_out: bfloat16 [4096, 5120], P('fsdp'), may hold values from -0.09375 to 0.09375
- cache_keys: bfloat16 [16384, 4096], P('frame', 'fsdp'), may hold values from -220 to 220
- cache_values: bfloat16 [16384, 4096], P('frame', 'fsdp'), may hold values from -6 to 6
- fresh_frame: bfloat16 [512, 5120], P('fsdp'), may hold values from -6 to 6
Outputs:
- next_window: bfloat16 [8, 512, 5120], P('frame', 'fsdp')
- finished: bfloat16 [512, 5120], P('fsdp')
- new_cache_keys: bfloat16 [16384, 4096], P('frame', 'fsdp')
- new_cache_values: bfloat16 [16384, 4096], P('frame', 'fsdp')
Inputs may be any that keep to these rules, and one draw needn't show every extreme that they name: Rows of the cache from cache_len on are unused.
All inputs are finite; a program needn't handle non-finite values.
Results may differ from a plain program's by a relative error of at most 0.015.
The roundings to bfloat16 on the way count: a program that leaves them out, or rounds other values in their place, can miss the bound.
Values may be sent and summed in bfloat16 or wider, within the bound.
No kernel may reach another device: no remote copies, remote signals or barrier semaphores. Data moves between devices by JAX's collectives and lax.ppermute only.
A program may use at most 128 MiB of HBM per device.

v0:
```python
import math

import jax
import jax.numpy as jnp
from jax import lax
from jax.experimental import pallas as pl
from jax.experimental.pallas import tpu as pltpu
from jax.sharding import Mesh
from jax.sharding import PartitionSpec as P

HD = 128
D = 5120
FT = 512
TOK = 16
ROWS = FT // 4
HALF = D // 2
EPS = 1e-06
NEG = -1e30
LOG2E = math.log2(math.e)
EXP_SCALE = LOG2E / math.sqrt(HD)
CHUNK = 1024
PAY = FT + 16

FRAME = ("zh", "core")
FSDP = ("x", "zl", "y")

ROOM = pltpu.CompilerParams(vmem_limit_bytes=18 << 20)


DIMS = (("x", 1, 4), ("x", 3, 4), ("zl", 1, 2), ("y", 1, 4), ("y", 3, 4))


def held_near(*blocks):
    return [pltpu.with_memory_space_constraint(b, pltpu.VMEM) for b in blocks]


def across(block, dim):
    axis, mask, size = DIMS[dim]
    return lax.ppermute(block, axis, [(i, i ^ mask) for i in range(size)])


def across_each(block, by_core):
    pairs = []
    for core in range(2):
        axis, mask, _ = DIMS[by_core[core]]
        for x in range(4):
            for zl in range(2):
                for y in range(4):
                    at = {"x": x, "zl": zl, "y": y}
                    to = dict(at, **{axis: at[axis] ^ mask})
                    pairs.append(
                        tuple(((core * 4 + p["x"]) * 2 + p["zl"]) * 4 + p["y"] for p in (at, to))
                    )
    return lax.ppermute(block, ("core", "x", "zl", "y"), pairs)


def frame_shift(block, distance):
    return lax.ppermute(block, FRAME, [(i, (i + distance) % 8) for i in range(8)])


def other_core(block):
    return lax.ppermute(block, "core", [(0, 1), (1, 0)])


def pieces_of(value):
    high = value.astype(jnp.bfloat16).astype(jnp.float32)
    rest = value - high
    middle = rest.astype(jnp.bfloat16).astype(jnp.float32)
    return high, middle, rest - middle


def norm_body(window_ref, condition_ref, out_ref, carry_ref):
    rows = window_ref[0].astype(jnp.float32)
    center = rows - jnp.mean(rows, axis=-1, keepdims=True)
    spread = jnp.mean(center * center, axis=-1, keepdims=True)
    out_ref[...] = (
        center * lax.rsqrt(spread + EPS) * (1.0 + condition_ref[1:2, :]) + condition_ref[0:1, :]
    ).astype(jnp.bfloat16)
    carry_ref[:TOK, :] = window_ref[0]
    gate = pieces_of(condition_ref[2:3, :])
    empty = jnp.zeros((TOK - 3, D), jnp.float32)
    carry_ref[TOK:, :] = jnp.concatenate([*gate, empty], axis=0).astype(jnp.bfloat16)


def normalise(window, condition):
    return pl.pallas_call(
        norm_body,
        out_shape=[
            pltpu.VMEM((TOK, D), jnp.bfloat16),
            pltpu.VMEM((2 * TOK, D), jnp.bfloat16),
        ],
        compiler_params=ROOM,
        name="normalise",
    )(window, condition)


def halves_body(*refs):
    blocks, outs = refs[:-2], refs[-2:]
    for i, block in enumerate(blocks):
        for h in range(2):
            outs[h][i * TOK : (i + 1) * TOK, :] = block[:, h * HALF : (h + 1) * HALF]


def halves(mine, got):
    return pl.pallas_call(
        halves_body,
        out_shape=[pltpu.VMEM((2 * TOK, HALF), jnp.bfloat16)] * 2,
        compiler_params=ROOM,
        name="halves",
    )(*held_near(mine, got))


def join_body(*refs):
    rows = refs[0].shape[0]
    for h in range(2):
        for i in range(4):
            refs[8 + h][i * rows : (i + 1) * rows, :] = refs[4 * h + i][...]


def join(first, second):
    shape = pltpu.VMEM((4 * first[0].shape[0], HALF), jnp.bfloat16)
    return pl.pallas_call(
        join_body, out_shape=[shape] * 2, compiler_params=ROOM, name="join"
    )(*held_near(*first, *second))


def after(block, *earlier):
    return lax.optimization_barrier((block, *earlier))[0]


def pick_body(core_ref, first_ref, second_ref, out_ref):
    @pl.when(core_ref[0] == 0)
    def _():
        out_ref[...] = first_ref[...]

    @pl.when(core_ref[0] != 0)
    def _():
        out_ref[...] = second_ref[...]


def pick(core, first, second):
    return pl.pallas_call(
        pick_body,
        in_specs=[pl.BlockSpec(memory_space=pltpu.SMEM)]
        + [pl.BlockSpec(memory_space=pltpu.VMEM)] * 2,
        out_shape=pltpu.VMEM(first.shape, first.dtype),
        compiler_params=ROOM,
        name="pick",
    )(core, *held_near(first, second))


def by_core(block, axis, routes):
    pairs = [(c * 4 + i, c * 4 + routes[c](i)) for c in range(2) for i in range(4)]
    return lax.ppermute(block, ("core", axis), pairs)


def ring(block, axis, core):
    before = lax.ppermute(block, axis, [(i, (i + 1) % 4) for i in range(4)])
    behind = lax.ppermute(block, axis, [(i, (i - 1) % 4) for i in range(4)])
    opposite = by_core(
        pick(core, before, behind), axis, (lambda i: (i + 1) % 4, lambda i: (i - 1) % 4)
    )
    return before, behind, opposite


def qkv_body(count, last, table, *refs):
    blocks, w_ref, refs, x_ref = refs[: 2 * count], refs[2 * count], refs[2 * count + 1 : -1], refs[-1]
    if last:
        before_ref, query_ref, key_value_ref, acc_ref = refs
    elif len(refs) == 2:
        before_ref, acc_ref = refs
    else:
        before_ref, acc_ref = None, refs[0]
    if before_ref is None:
        acc_ref[...] = jnp.zeros(acc_ref.shape, jnp.float32)
    else:
        acc_ref[...] = before_ref[...]
    for i in range(2 * count):
        x_ref[i] = blocks[i][...]

    def one(i, carry):
        at = pl.multiple_of((i % 2) * HALF, HALF)
        w = jnp.concatenate([w_ref[c, pl.ds(at, HALF), :] for c in range(3)], axis=1)
        product = jnp.dot(x_ref[i], w, preferred_element_type=jnp.float32)
        for j in range(8):
            at = pl.multiple_of(table[i * 8 + j] * TOK, TOK)
            acc_ref[pl.ds(at, TOK), :] += product[j * TOK : (j + 1) * TOK, :]
        return carry

    lax.fori_loop(0, 2 * count, one, 0)
    if last:
        query_ref[...] = acc_ref[:, :HD].astype(jnp.bfloat16)
        key_value_ref[...] = acc_ref[:, HD:].astype(jnp.bfloat16)


def qkv_add(table, pairs, w_qkv, before, last):
    count = len(pairs)
    acc = pltpu.VMEM((FT, 3 * HD), jnp.float32)
    operands = held_near(*[b for pair in pairs for b in pair])
    operands += [w_qkv] + ([] if before is None else held_near(before))
    outs = [
        pltpu.VMEM((FT, HD), jnp.bfloat16),
        pltpu.VMEM((FT, 2 * HD), jnp.bfloat16),
    ]
    return pl.pallas_call(
        lambda *refs: qkv_body(count, last, *refs),
        in_specs=[pl.BlockSpec(memory_space=pltpu.SMEM)]
        + [pl.BlockSpec(memory_space=pltpu.VMEM)] * len(operands),
        out_shape=outs if last else acc,
        scratch_shapes=([pltpu.VMEM(acc.shape, jnp.float32)] if last else [])
        + [pltpu.VMEM((2 * count, ROWS, HALF), jnp.bfloat16)],
        cost_estimate=pl.CostEstimate(
            flops=2 * count * ROWS * D * 3 * HD, bytes_accessed=6 << 20, transcendentals=0
        ),
        compiler_params=ROOM,
        name="qkv_last" if last else "qkv_add",
    )(table, *operands)


def places(x, y, pieces):
    odd = {"x": x % 2 == 1, "y": y % 2 == 1}
    bits = {"x": (16, 8), "y": (2, 1)}

    def place(axis, piece):
        one, three = bits[axis]
        if piece == 0:
            return 0
        if piece == 3:
            return one + three
        return jnp.where(odd[axis] == (piece == 1), one, three)

    table = []
    for piece in pieces:
        for near, far in (("x", "y"), ("y", "x")):
            for j in range(8):
                table.append(place(far, piece) + place(near, j // 2) + 4 * (j % 2))
    return jnp.stack([jnp.asarray(t, jnp.int32) for t in table])


def attention_body(count, limits, *refs):
    qs, (k0, v0, cache1, kv0, kv1) = refs[:count], refs[count : count + 5]
    outs, stat_ref = refs[count + 5 : 2 * count + 5], refs[-1]
    chunks = []
    for c, (k, v, side) in enumerate(((k0, v0, 0), (cache1, cache1, HD))):
        for at in range(0, k.shape[0], CHUNK):
            chunks.append((k, v, side, at, c))
    chunks.append((None, None, 0, 0, 2))
    rows = 256
    blocks = FT // rows
    ones = jnp.ones((CHUNK, HD), jnp.bfloat16)

    def one_block(index, carry):
        frame = index // blocks
        start = pl.multiple_of((index % blocks) * rows, rows)
        limit = [limits[frame * 4 + c] for c in range(4)]
        any_key = (limit[0] > 0) | (limit[1] > 0) | (limit[2] > 0) | (limit[3] > 0)
        q = qs[0][pl.ds(start, rows), :]
        for f in range(1, count):
            q = jnp.where(frame == f, qs[f][pl.ds(start, rows), :], q)
        peak = jnp.full((rows, 1), NEG, jnp.float32)
        acc = jnp.zeros((rows, 2 * HD), jnp.float32)
        column = lax.broadcasted_iota(jnp.int32, (1, CHUNK), 1)
        for k, v, side, at, c in chunks:
            if k is None:
                keys, values = (
                    jnp.concatenate([kv[:, h : h + HD] for kv in (kv0, kv1)], axis=0)
                    for h in (0, HD)
                )
                inside = column < jnp.where(column < FT, limit[2], FT + limit[3])
            else:
                keys, values = k[at : at + CHUNK, :HD], v[at : at + CHUNK, side : side + HD]
                inside = column < limit[c] - at
            s = lax.dot_general(
                q, keys, (((1,), (1,)), ((), ())), preferred_element_type=jnp.float32
            )
            s = jnp.where(inside, s, NEG)
            newest = jnp.maximum(peak, jnp.max(s, axis=-1, keepdims=True))
            w = jnp.exp2((s - newest) * EXP_SCALE).astype(jnp.bfloat16)
            values = jnp.concatenate([values, ones], axis=1)
            acc = acc * jnp.exp2((peak - newest) * EXP_SCALE) + jnp.dot(
                w, values, preferred_element_type=jnp.float32
            )
            peak = newest
        total = acc[:, HD:]
        result = jnp.where(any_key, acc[:, :HD] / total, 0.0).astype(jnp.bfloat16)
        for f in range(count):

            @pl.when(frame == f)
            def _(f=f):
                outs[f][pl.ds(start, rows), :] = result

        level = jnp.where(any_key, peak * EXP_SCALE + jnp.log2(total), NEG)
        stat_ref[pl.ds(index, 1), :] = level.T[0:1, :]
        return carry

    lax.fori_loop(0, count * blocks, one_block, 0)
    for f in range(count):
        flat = jnp.concatenate(
            [stat_ref[i : i + 1, :] for i in range(f * blocks, (f + 1) * blocks)], axis=1
        )
        lines = []
        for piece in pieces_of(flat):
            for at in range(0, FT, HD):
                lines.append(piece[:, at : at + HD])
        lines.append(jnp.zeros((4, HD), jnp.float32))
        outs[f][FT:, :] = jnp.concatenate(lines, axis=0).astype(jnp.bfloat16)


def attention(limits, qs, k0, v0, cache1, kv0, kv1):
    count = len(qs)
    whole = pl.BlockSpec(memory_space=pltpu.VMEM)
    return pl.pallas_call(
        lambda *refs: attention_body(count, *refs),
        in_specs=[pl.BlockSpec(memory_space=pltpu.SMEM)] + [whole] * (5 + count),
        out_shape=[pltpu.VMEM((PAY, HD), jnp.bfloat16)] * count,
        scratch_shapes=[pltpu.VMEM((8, 256), jnp.float32)],
        cost_estimate=pl.CostEstimate(
            flops=count * 4 * FT * 5120 * HD,
            bytes_accessed=3 << 20,
            transcendentals=count * FT * 5120,
        ),
        compiler_params=ROOM,
        name="attention",
    )(limits, *qs, k0, v0, cache1, kv0, kv1)


def combine_body(*refs):
    parts, o_ref = refs[:-1], refs[-1]
    levels = []
    for part in parts:
        lines = part[FT:, :].astype(jnp.float32)
        level = (lines[0:4] + lines[4:8]) + lines[8:12]
        row = jnp.concatenate([level[i : i + 1, :] for i in range(4)], axis=1)
        levels.append(jnp.broadcast_to(row, (HD, FT)).T)
    peak = levels[0]
    for level in levels[1:]:
        peak = jnp.maximum(peak, level)
    total = jnp.zeros((FT, HD), jnp.float32)
    acc = jnp.zeros((FT, HD), jnp.float32)
    for part, level in zip(parts, levels):
        w = jnp.exp2(level - peak)
        total = total + w
        acc = acc + w * part[:FT, :].astype(jnp.float32)
    o_ref[...] = (acc / total).astype(jnp.bfloat16)


def combine(parts):
    return pl.pallas_call(
        combine_body,
        out_shape=pltpu.VMEM((FT, HD), jnp.bfloat16),
        compiler_params=ROOM,
        name="combine",
    )(*held_near(*parts))


def beside_body(keys_ref, values_ref, out_ref):
    out_ref[:, :HD] = keys_ref[...]
    out_ref[:, HD:] = values_ref[...]


def beside(keys, values):
    return pl.pallas_call(
        beside_body,
        out_shape=pltpu.VMEM((keys.shape[0], 2 * HD), keys.dtype),
        compiler_params=ROOM,
        name="beside",
    )(keys, values)


def insert_body(offset_ref, root_ref, k_ref, v_ref, new_k_ref, new_v_ref, rolled_ref):
    new_k_ref[...] = k_ref[...]
    new_v_ref[...] = v_ref[...]
    offset = offset_ref[0]
    rest = offset & (TOK - 1)
    base = offset - rest
    rows = jnp.concatenate(
        [root_ref[...].astype(jnp.float32), jnp.zeros((TOK, 2 * HD), jnp.float32)], axis=0
    )
    rolled_ref[...] = pltpu.roll(rows, rest, 0)

    def one(i, carry):
        start = base + i * TOK

        @pl.when((start >= 0) & (start < k_ref.shape[0]))
        def _():
            at = pl.ds(pl.multiple_of(start, TOK), TOK)
            source = pl.multiple_of(i * TOK, TOK)
            row = source + lax.broadcasted_iota(jnp.int32, (TOK, HD), 0)
            inside = (row >= rest) & (row < rest + FT)
            for c, out in enumerate((new_k_ref, new_v_ref)):
                fresh = rolled_ref[pl.ds(source, TOK), c * HD : (c + 1) * HD]
                out[at, :] = jnp.where(inside, fresh, out[at, :].astype(jnp.float32)).astype(
                    out.dtype
                )

        return carry

    lax.fori_loop(0, FT // TOK + 1, one, 0)


def insert_rows(root, keys, values, offset):
    return pl.pallas_call(
        insert_body,
        in_specs=[pl.BlockSpec(memory_space=pltpu.SMEM)]
        + [pl.BlockSpec(memory_space=pltpu.VMEM)] * 3,
        out_shape=[jax.ShapeDtypeStruct(keys.shape, keys.dtype)] * 2,
        scratch_shapes=[pltpu.VMEM((FT + TOK, 2 * HD), jnp.float32)],
        compiler_params=ROOM,
        name="insert_rows",
    )(offset, *held_near(root), keys, values)


def order_body(table, own_ref, other_ref, first_ref, second_ref, out_ref):
    slot = table[32]
    for source, chosen in (
        (own_ref, slot == 0),
        (other_ref, slot == 1),
        (first_ref, (slot == 2) | (slot == 7)),
        (second_ref, (slot > 2) & (slot < 7)),
    ):

        @pl.when(chosen)
        def _(source=source):
            for j in range(32):
                at = pl.multiple_of(table[j] * TOK, TOK)
                out_ref[j * TOK : (j + 1) * TOK, :] = source[pl.ds(at, TOK), :]


def token_places(slot, x, zl, y):
    block = jnp.arange(32, dtype=jnp.int32)

    def pair(apart):
        three = (apart >> 1) & 1
        return ((apart ^ (3 * three)) & 1) * 2 + three

    place = (
        pair((block >> 3) ^ x) * 8 + (((block >> 2) & 1) ^ zl) * 4 + pair((block & 3) ^ y)
    )
    return jnp.concatenate([place, slot.reshape(1)]).astype(jnp.int32)


def in_token_order(table, own, other, first, second):
    return pl.pallas_call(
        order_body,
        in_specs=[pl.BlockSpec(memory_space=pltpu.SMEM)]
        + [pl.BlockSpec(memory_space=pltpu.VMEM)] * 4,
        out_shape=pltpu.VMEM(own.shape, own.dtype),
        compiler_params=ROOM,
        name="in_token_order",
    )(table, own, other, first, second)


def relay_body(slot_ref, own_ref, other_ref, got_ref, out_ref):
    for source, chosen in (
        (own_ref, slot_ref[0] == 0),
        (other_ref, slot_ref[0] == 1),
        (got_ref, slot_ref[0] > 1),
    ):

        @pl.when(chosen)
        def _(source=source):
            out_ref[...] = source[...]


def relay(slot, own, other, got):
    return pl.pallas_call(
        relay_body,
        in_specs=[pl.BlockSpec(memory_space=pltpu.SMEM)]
        + [pl.BlockSpec(memory_space=pltpu.VMEM)] * 3,
        out_shape=pltpu.VMEM(own.shape, own.dtype),
        compiler_params=ROOM,
        name="relay",
    )(slot, own, other, got)


REDUCE = ((2, 3), (3, 4), (4, 2))


def stack_body(*refs):
    for i in range(3):
        refs[3][i * HD : (i + 1) * HD, :] = refs[i][...]


def stack(blocks):
    return pl.pallas_call(
        stack_body,
        out_shape=pltpu.VMEM((3 * HD, HALF), jnp.bfloat16),
        compiler_params=ROOM,
        name="stack",
    )(*held_near(*blocks))


def out_body(order, t0, t1, t2, t3, n0, n1, n2, n3, f0, f1, keep_ref, send_ref, lhs_ref):
    for b in range(8):
        block = pl.multiple_of(order[b] * TOK, TOK)
        lhs_ref[b * TOK : (b + 1) * TOK, :] = jnp.concatenate(
            [t[pl.ds(block, TOK), :] for t in (t0, t1, t2, t3)], axis=1
        )
    for c, side in enumerate(((n0, n1, n2, n3), (f0, f1))):
        columns = slice(c * HALF, (c + 1) * HALF)
        weights = jnp.concatenate([w[...] for w in side], axis=0)
        product = jnp.dot(lhs_ref[...], weights, preferred_element_type=jnp.float32)
        keep_ref[:, columns] = product[: ROWS // 2].astype(jnp.bfloat16)
        send_ref[:, columns] = product[ROWS // 2 :].astype(jnp.bfloat16)


def out_project(order, tokens, sides):
    return pl.pallas_call(
        out_body,
        in_specs=[pl.BlockSpec(memory_space=pltpu.SMEM)]
        + [pl.BlockSpec(memory_space=pltpu.VMEM)] * 10,
        out_shape=[pltpu.VMEM((ROWS // 2, D), jnp.bfloat16)] * 2,
        scratch_shapes=[pltpu.VMEM((ROWS, 4 * HD), jnp.bfloat16)],
        compiler_params=ROOM,
        name="out_project",
    )(order, *held_near(*tokens), *sides)


def add_body(keep_ref, got_ref, next_keep_ref, next_send_ref):
    total = keep_ref[...].astype(jnp.float32) + got_ref[...].astype(jnp.float32)
    rows = total.shape[0] // 2
    next_keep_ref[...] = total[:rows].astype(jnp.bfloat16)
    next_send_ref[...] = total[rows:].astype(jnp.bfloat16)


def add_up(keep, got):
    shape = pltpu.VMEM((keep.shape[0] // 2, D), jnp.bfloat16)
    return pl.pallas_call(
        add_body, out_shape=[shape] * 2, compiler_params=ROOM, name="add_up"
    )(*held_near(keep, got))


def finish_body(core_ref, keep_ref, got_ref, carry_ref, out_ref):
    total = keep_ref[...].astype(jnp.float32) + got_ref[...].astype(jnp.float32)
    near, far = total[:, :HALF], total[:, HALF:]
    lines = carry_ref[TOK:, :].astype(jnp.float32)
    gate = (lines[0:1] + lines[1:2]) + lines[2:3]
    base = carry_ref[:TOK, :].astype(jnp.float32)
    first = core_ref[0] == 0
    for h, product in ((0, jnp.where(first, near, far)), (1, jnp.where(first, far, near))):
        columns = slice(h * HALF, (h + 1) * HALF)
        out_ref[:, columns] = (base[:, columns] + gate[:, columns] * product).astype(jnp.bfloat16)


def finish(core, keep, got, carry):
    return pl.pallas_call(
        finish_body,
        in_specs=[pl.BlockSpec(memory_space=pltpu.SMEM)]
        + [pl.BlockSpec(memory_space=pltpu.VMEM)] * 3,
        out_shape=pltpu.VMEM((TOK, D), jnp.bfloat16),
        compiler_params=ROOM,
        name="finish",
    )(core, *held_near(keep, got, carry))


def step(
    window,
    levels,
    actions,
    cache_len,
    level_table,
    action_table,
    w_qkv,
    w_out,
    cache_keys,
    cache_values,
    fresh_frame,
):
    core = lax.axis_index("core")
    slot = lax.axis_index(FRAME)
    length = cache_len[0]
    shard_rows = cache_keys.shape[0]

    condition = (
        lax.dynamic_slice_in_dim(level_table, levels[0], 1, 0)
        + lax.dynamic_slice_in_dim(action_table, actions[0], 1, 0)
    )[0]
    normed, carry = normalise(window, condition)

    got = across(normed, 2)

    places_here = [lax.axis_index(a).astype(jnp.int32) for a in FSDP]
    slot, core, length, w_late, x, zl, y, _ = lax.optimization_barrier(
        (slot, core, length, w_out, *places_here, normed)
    )
    slots = slot.astype(jnp.int32).reshape(1)
    cores = core.astype(jnp.int32).reshape(1)
    offset = (length - slot * shard_rows).astype(jnp.int32)
    w_near = lax.dynamic_slice_in_dim(w_late, core * HALF, HALF, 1)
    w_far = lax.dynamic_slice_in_dim(w_late, (1 - core) * HALF, HALF, 1)

    def limits(*ahead):
        rows = []
        for steps in ahead:
            frame = (slot + steps) % 8
            partner = slot ^ 1
            rows += [
                length - slot * shard_rows,
                length - partner * shard_rows,
                jnp.where(slot <= frame, FT, 0),
                jnp.where(partner <= frame, FT, 0),
            ]
        return jnp.stack(rows).astype(jnp.int32)

    tables = [places(x, y, p) for p in ((0,), (1, 2), (3,))]
    tables += [limits(0), limits(2, 6), limits(4), token_places(slots[0], x, zl, y)]
    tables += [
        jnp.where(
            core == 0,
            jnp.arange(8, dtype=jnp.int32),
            jnp.array([(b & 1) * 4 + (b >> 1) for b in range(8)], jnp.int32),
        ),
        jnp.clip(offset, -FT, shard_rows).reshape(1),
        cores,
        slots,
    ]
    got, w_near, w_far, *tables = lax.optimization_barrier((got, w_near, w_far, *tables))
    order, offset, cores, slots = tables[7:]
    first, second = halves(normed, got)
    first, second = join((first, *ring(first, "x", cores)), (second, *ring(second, "y", cores)))

    late = lax.optimization_barrier((first, second, cache_keys, cache_values))
    first, second = late[:2]
    other_cache = other_core(beside(late[2], late[3]))

    around = list(zip(ring(first, "y", cores), ring(second, "x", cores)))
    acc = qkv_add(tables[0], [(first, second)], w_qkv, None, False)
    acc = qkv_add(tables[1], around[:2], w_qkv, acc, False)
    acc, opposite, other_cache = lax.optimization_barrier((acc, around[2], other_cache))
    query, key_value = qkv_add(tables[2], [opposite], w_qkv, acc, True)

    q_up = frame_shift(query, -2)
    q_down = frame_shift(query, 2)
    q_far = frame_shift(query, 4)
    other_key_value = other_core(key_value)

    def attend(table, *queries):
        return attention(
            table,
            queries,
            cache_keys,
            cache_values,
            other_cache,
            key_value,
            other_key_value,
        )

    (part,) = attend(tables[3], query)
    part, q_up, q_down, w_next, carry = lax.optimization_barrier(
        (part, q_up, q_down, w_near, carry)
    )
    sent = [frame_shift(part, -1)]
    w_one, w_three = across(w_next, 0), across(w_next, 1)
    other_late = after(other_key_value, part)
    root_first = lax.ppermute(
        relay(slots, key_value, other_late, key_value), FRAME, [(0, 2), (1, 7)]
    )
    part_up, part_down = attend(tables[4], q_up, q_down)
    sent.append(frame_shift(part_up, 1))
    sent.append(frame_shift(part_down, -3))
    part_up, q_far, w_one, w_three, root_first = lax.optimization_barrier(
        (part_up, q_far, w_one, w_three, root_first)
    )
    w_two = by_core(pick(cores, w_one, w_three), "x", (lambda i: i ^ 3, lambda i: i ^ 1))
    (part,) = attend(tables[5], q_far)
    sent.append(frame_shift(part, 3))
    part, w_two = lax.optimization_barrier((part, w_two))
    heads_far = other_core(stack((w_one, w_three, w_two)))
    sides = [w_near, w_one, w_three, w_two, w_far, heads_far]
    carry_next = frame_shift(after(carry, part), -1)

    attended = combine(sent).reshape(2, 2, ROWS, HD)

    beyond = lax.ppermute(attended[1, 1], "x", [(i, i ^ 2) for i in range(4)])
    together = [attended[0, 0], across(attended[1, 0], 0), across(attended[0, 1], 1), beyond]
    keep, send = out_project(order, together, sides)
    got = across_each(send, REDUCE[0])
    root_second = lax.ppermute(
        relay(slots, key_value, other_key_value, after(root_first, send)),
        FRAME,
        [(0, 4), (1, 5), (2, 3), (7, 6)],
    )
    keep, send = add_up(keep, got)
    got = across_each(send, REDUCE[1])
    got, root_second = lax.optimization_barrier((got, root_second))
    keep, send = add_up(keep, got)
    got = across_each(send, REDUCE[2])
    root = in_token_order(tables[6], key_value, other_key_value, root_first, root_second)
    got, root = lax.optimization_barrier((got, root))
    updated = finish(cores, keep, got, carry_next)

    next_window = jnp.where(slot == 7, fresh_frame, updated)
    arrived = [lax.ppermute(updated, FRAME, [(7, 2 * chip + 1)]) for chip in (1, 0, 2)]
    new_keys, new_values = insert_rows(
        after(root, updated), cache_keys, cache_values, offset
    )
    arrived, new_keys, new_values = lax.optimization_barrier((arrived, new_keys, new_values))
    finished = jnp.where(slot == 7, updated, arrived[0] + arrived[1] + arrived[2])
    finished = jnp.where(core == 0, lax.ppermute(finished, "core", [(1, 0)]), finished)
    return (next_window[None], finished, new_keys, new_values)


def solution(mesh):
    split = Mesh(mesh.devices.reshape(4, 2, 4, 2, 4), FRAME + FSDP)
    return jax.shard_map(
        step,
        mesh=split,
        in_specs=(
            P(FRAME, FSDP, None),
            P(FRAME),
            P(FRAME),
            P(),
            P(),
            P(),
            P(None, None, FSDP),
            P(FSDP, None),
            P(FRAME, FSDP),
            P(FRAME, FSDP),
            P(FSDP, None),
        ),
        out_specs=(P(FRAME, FSDP, None), P(FSDP, None), P(FRAME, FSDP), P(FRAME, FSDP)),
        check_vma=False,
    )
```

profile of v0, /device:TPU:1, one launch (start us, length us, event | category | flops | bytes accessed | tf_op | source)
XLA Modules:
  0.0 174.7 jit_solution(12643756539769685615)
XLA Ops:
  5.2 2.5 %collective-permute-start = (bf16[16,5120]{1,0:T(8,128)(2,1)S(1)}, bf16[16,5120]{1,0:T(8,128)(2,1)}, u32[]{:S(2)}, u32[]{:S(2)}) collective-permute-start(bf16[16,5120]{1,0:T(8,128)(2,1)S(1)} %get-tuple-element.73.refs_0_), channel_id=1, source_target_pairs={{0,4},{4,0},{1,5},{5,1},{2,6},{6,2},{3,7},{7,3},{8,12},{12,8},{9,1... | collective-permute-start | bytes 491528 | tf_op jit(solution)/shard_map/ppermute | solution.py:39
  8.4 1.4 constant_dynamic-slice_fusion
  12.1 1.8 %collective-permute-start.1 = (bf16[32,2560]{1,0:T(8,128)(2,1)S(1)}, bf16[32,2560]{1,0:T(8,128)(2,1)S(1)}, u32[]{:S(2)}, u32[]{:S(2)}) collective-permute-start(bf16[32,2560]{1,0:T(8,128)(2,1)S(1)} %get-tuple-element.87.refs_0_), channel_id=1, source_target_pairs={{0,8},{8,16},{16,24},{24,0},{1,9},{9,17},{17,25},{25,1},{2,10},{10... | collective-permute-start | bytes 491528 | tf_op jit(solution)/shard_map/ppermute | solution.py:158
  13.8 1.4 collective-permute-start.2
  15.2 1.4 collective-permute-start.4
  16.6 1.4 collective-permute-start.5
  18.1 2.6 %collective-permute-start.3 = (bf16[32,2560]{1,0:T(8,128)(2,1)S(1)}, bf16[32,2560]{1,0:T(8,128)(2,1)S(1)}, u32[]{:S(2)}, u32[]{:S(2)}) collective-permute-start(bf16[32,2560]{1,0:T(8,128)(2,1)S(1)} %pick.5), channel_id=1, source_target_pairs={{0,8},{8,16},{16,24},{24,0},{32,56},{40,32},{48,40},{56,48},{1,9},... | collective-permute-start | bytes 491528 | tf_op jit(solution)/shard_map/ppermute | solution.py:154
  21.0 2.6 %collective-permute-start.6 = (bf16[32,2560]{1,0:T(8,128)(2,1)S(1)}, bf16[32,2560]{1,0:T(8,128)(2,1)S(1)}, u32[]{:S(2)}, u32[]{:S(2)}) collective-permute-start(bf16[32,2560]{1,0:T(8,128)(2,1)S(1)} %pick.6), channel_id=1, source_target_pairs={{0,1},{1,2},{2,3},{3,0},{32,35},{33,32},{34,33},{35,34},{4,5},{5,6... | collective-permute-start | bytes 491528 | tf_op jit(solution)/shard_map/ppermute | solution.py:154
  23.6 2.3 %collective-permute-done.6.refs_7_ = bf16[32,2560]{1,0:T(8,128)(2,1)S(1)} collective-permute-done((bf16[32,2560]{1,0:T(8,128)(2,1)S(1)}, bf16[32,2560]{1,0:T(8,128)(2,1)S(1)}, u32[]{:S(2)}, u32[]{:S(2)}) %collective-permute-start.6) | collective-permute-done | bytes 163872 | tf_op jit(solution)/shard_map/ppermute | solution.py:154
  27.1 2.5 %collective-permute-start.9 = (bf16[128,2560]{1,0:T(8,128)(2,1)S(1)}, bf16[128,2560]{1,0:T(8,128)(2,1)S(1)}, u32[]{:S(2)}, u32[]{:S(2)}) collective-permute-start(bf16[128,2560]{1,0:T(8,128)(2,1)S(1)} %get-tuple-element.91.refs_1_), channel_id=1, source_target_pairs={{0,3},{1,0},{2,1},{3,2},{4,7},{5,4},{6,5},{7,6},{8,11},{9,8},{10,9... | collective-permute-start | bytes 1966088 | tf_op jit(solution)/shard_map/ppermute | solution.py:159
  29.5 2.7 %collective-permute-start.10 = (bf16[128,2560]{1,0:T(8,128)(2,1)S(1)}, bf16[128,2560]{1,0:T(8,128)(2,1)S(1)}, u32[]{:S(2)}, u32[]{:S(2)}) collective-permute-start(bf16[128,2560]{1,0:T(8,128)(2,1)S(1)} %get-tuple-element.92.refs_2_), channel_id=1, source_target_pairs={{0,24},{8,0},{16,8},{24,16},{1,25},{9,1},{17,9},{25,17},{2,26},{10... | collective-permute-start | bytes 1966088 | tf_op jit(solution)/shard_map/ppermute | solution.py:159
  32.4 6.0 %collective-permute-start.13 = (bf16[2048,256]{1,0:T(8,128)(2,1)S(1)}, bf16[2048,256]{1,0:T(8,128)(2,1)S(1)}, u32[]{:S(2)}, u32[]{:S(2)}) collective-permute-start(bf16[2048,256]{1,0:T(8,128)(2,1)S(1)} %beside.1), channel_id=1, source_target_pairs={{0,32},{32,0},{1,33},{33,1},{2,34},{34,2},{3,35},{35,3},{4,36},{36... | collective-permute-start | bytes 3145736 | tf_op jit(solution)/shard_map/ppermute | solution.py:62
  38.4 1.4 collective-permute-done.7.refs_1_.first_ref
  39.8 2.7 %collective-permute-start.11 = (bf16[128,2560]{1,0:T(8,128)(2,1)S(1)}, bf16[128,2560]{1,0:T(8,128)(2,1)S(1)}, u32[]{:S(2)}, u32[]{:S(2)}) collective-permute-start(bf16[128,2560]{1,0:T(8,128)(2,1)S(1)} %pick.7), channel_id=1, source_target_pairs={{0,1},{1,2},{2,3},{3,0},{32,35},{33,32},{34,33},{35,34},{4,5},{5,6... | collective-permute-start | bytes 1966088 | tf_op jit(solution)/shard_map/ppermute | solution.py:154
  42.6 1.8 %collective-permute-start.12 = (bf16[128,2560]{1,0:T(8,128)(2,1)S(1)}, bf16[128,2560]{1,0:T(8,128)(2,1)S(1)}, u32[]{:S(2)}, u32[]{:S(2)}) collective-permute-start(bf16[128,2560]{1,0:T(8,128)(2,1)S(1)} %pick.8), channel_id=1, source_target_pairs={{0,8},{8,16},{16,24},{24,0},{32,56},{40,32},{48,40},{56,48},{1,9},... | collective-permute-start | bytes 1966088 | tf_op jit(solution)/shard_map/ppermute | solution.py:154
  44.4 1.8 %qkv_add.2.refs_6_ = f32[512,384]{1,0:T(8,128)S(1)} custom-call(s32[16]{0:T(128)S(1)} %stack.159.refs_0_, bf16[128,2560]{1,0:T(8,128)(2,1)S(1)} %get-tuple-element.91.refs_1_, bf16[128,2560]{1,0:T(8,128)(2,1)S(1)} %get-tuple-element.92.refs_2_, bf16[3,5120,128]{2,1,0:T(8,128)(2,1)S(1)} %copy-done.1), custom_call_target="tpu_custom_call" | custom-call | flops 503316480 | bytes 6291456 | tf_op jit(solution)/shard_map/qkv_add/pallas_call | solution.py:205
  46.2 2.9 %qkv_add.3.refs_4_ = f32[512,384]{1,0:T(8,128)S(1)} custom-call(s32[32]{0:T(128)S(1)} %stack.176.refs_0_, bf16[128,2560]{1,0:T(8,128)(2,1)S(1)} %collective-permute-done.7.refs_1_.first_ref, bf16[128,2560]{1,0:T(8,128)(2,1)S(1)} %collective-permute-done.8.refs_2_.first_ref, bf16[128,2560]{1,0:T(8,128)(2,1)S(1)} %collective-permute-done.9.refs_3_.second_ref, ...), custom_call_target="tpu_custom_call" | custom-call | flops 1006632960 | bytes 6291456 | tf_op jit(solution)/shard_map/qkv_add/pallas_call | solution.py:205
  49.1 2.0 %collective-permute-done.11.refs_1_ = bf16[128,2560]{1,0:T(8,128)(2,1)S(1)} collective-permute-done((bf16[128,2560]{1,0:T(8,128)(2,1)S(1)}, bf16[128,2560]{1,0:T(8,128)(2,1)S(1)}, u32[]{:S(2)}, u32[]{:S(2)}) %collective-permute-start.11) | collective-permute-done | bytes 655392 | tf_op jit(solution)/shard_map/ppermute | solution.py:154
  51.1 2.7 %collective-permute-done.12.refs_2_ = bf16[128,2560]{1,0:T(8,128)(2,1)S(1)} collective-permute-done((bf16[128,2560]{1,0:T(8,128)(2,1)S(1)}, bf16[128,2560]{1,0:T(8,128)(2,1)S(1)}, u32[]{:S(2)}, u32[]{:S(2)}) %collective-permute-start.12) | collective-permute-done | bytes 655392 | tf_op jit(solution)/shard_map/ppermute | solution.py:154
  53.8 1.8 %qkv_last.1 = (bf16[512,128]{1,0:T(8,128)(2,1)S(1)}, bf16[512,256]{1,0:T(8,128)(2,1)S(1)}) custom-call(s32[16]{0:T(128)S(1)} %stack.177.refs_0_, bf16[128,2560]{1,0:T(8,128)(2,1)S(1)} %collective-permute-done.11.refs_1_, bf16[128,2560]{1,0:T(8,128)(2,1)S(1)} %collective-permute-done.12.refs_2_, bf16[3,5120,128]{2,1,0:T(8,128)(2,1)S(1)} %copy-done.1, ...), custom_call_target="tpu_custom_call" | custom-call | flops 503316480 | bytes 6291456 | tf_op jit(solution)/shard_map/qkv_last/pallas_call | solution.py:205
  55.6 7.9 %collective-permute-start.14 = (bf16[512,256]{1,0:T(8,128)(2,1)S(1)}, bf16[512,256]{1,0:T(8,128)(2,1)S(1)}, u32[]{:S(2)}, u32[]{:S(2)}) collective-permute-start(bf16[512,256]{1,0:T(8,128)(2,1)S(1)} %get-tuple-element.101.refs_5_.refs_6_.own_ref.got_ref), channel_id=1, source_target_pairs={{0,32},{32,0},{1,33},{33,1},{2,34},{34,2},{3,35},{35,3},{4,36},{36... | collective-permute-start | bytes 786440 | tf_op jit(solution)/shard_map/ppermute | solution.py:62
  63.5 5.3 %collective-permute-start.15 = (bf16[512,128]{1,0:T(8,128)(2,1)S(1)}, bf16[512,128]{1,0:T(8,128)(2,1)S(1)}, u32[]{:S(2)}, u32[]{:S(2)}) collective-permute-start(bf16[512,128]{1,0:T(8,128)(2,1)S(1)} %get-tuple-element.99.refs_1_), channel_id=1, source_target_pairs={{0,192},{32,224},{64,0},{96,32},{128,64},{160,96},{192,128},{224,1... | collective-permute-start | bytes 393224 | tf_op jit(solution)/shard_map/ppermute | solution.py:58
  68.8 5.0 %attention.3 = bf16[528,128]{1,0:T(8,128)(2,1)S(1)} custom-call(s32[4]{0:T(128)S(1)} %get-tuple-element.83.refs_0_, bf16[512,128]{1,0:T(8,128)(2,1)S(1)} %get-tuple-element.99.refs_1_, bf16[2048,128]{1,0:T(8,128)(2,1)S(1)} %copy-done.2, bf16[2048,128]{1,0:T(8,128)(2,1)S(1)} %copy-done.3, bf16[2048,256]{1,0:T(8,128)(2,1)S(1)} %collective-permute-done.13.refs_4_.refs_5_, ...), custom_call_target="tpu_custom_call" | custom-call | flops 1342177280 | bytes 3145728 | tf_op jit(solution)/shard_map/attention/pallas_call | solution.py:312
  74.2 2.1 %collective-permute-done.16.refs_2_ = bf16[512,128]{1,0:T(8,128)(2,1)S(1)} collective-permute-done((bf16[512,128]{1,0:T(8,128)(2,1)S(1)}, bf16[512,128]{1,0:T(8,128)(2,1)S(1)}, u32[]{:S(2)}, u32[]{:S(2)}) %collective-permute-start.16) | collective-permute-done | bytes 131104 | tf_op jit(solution)/shard_map/ppermute | solution.py:58
  76.3 1.7 collective-permute-start.22
  78.1 4.3 %collective-permute-start.23 = (bf16[512,256]{1,0:T(8,128)(2,1)S(1)}, bf16[512,256]{1,0:T(8,128)(2,1)S(1)}, u32[]{:S(2)}, u32[]{:S(2)}) collective-permute-start(bf16[512,256]{1,0:T(8,128)(2,1)S(1)} %relay.2), channel_id=1, source_target_pairs={{0,64},{32,224},{1,65},{33,225},{2,66},{34,226},{3,67},{35,227},{4... | collective-permute-start | bytes 786440 | tf_op jit(solution)/shard_map/ppermute | solution.py:655
  82.5 9.5 %attention.4 = (bf16[528,128]{1,0:T(8,128)(2,1)S(1)}, bf16[528,128]{1,0:T(8,128)(2,1)S(1)}) custom-call(s32[8]{0:T(128)S(1)} %stack.187.refs_0_, bf16[512,128]{1,0:T(8,128)(2,1)S(1)} %collective-permute-done.15.refs_1_, bf16[512,128]{1,0:T(8,128)(2,1)S(1)} %collective-permute-done.16.refs_2_, bf16[2048,128]{1,0:T(8,128)(2,1)S(1)} %copy-done.2, ...), custom_call_target="tpu_custom_call" | custom-call | flops 2684354560 | bytes 3145728 | tf_op jit(solution)/shard_map/attention/pallas_call | solution.py:312
  92.0 1.8 %collective-permute-done.20.refs_1_ = bf16[512,128]{1,0:T(8,128)(2,1)S(1)} collective-permute-done((bf16[512,128]{1,0:T(8,128)(2,1)S(1)}, bf16[512,128]{1,0:T(8,128)(2,1)S(1)}, u32[]{:S(2)}, u32[]{:S(2)}) %collective-permute-start.20) | collective-permute-done | bytes 131104 | tf_op jit(solution)/shard_map/ppermute | solution.py:58
  95.3 5.0 %attention.5 = bf16[528,128]{1,0:T(8,128)(2,1)S(1)} custom-call(s32[4]{0:T(128)S(1)} %get-tuple-element.110.refs_0_, bf16[512,128]{1,0:T(8,128)(2,1)S(1)} %collective-permute-done.20.refs_1_, bf16[2048,128]{1,0:T(8,128)(2,1)S(1)} %copy-done.2, bf16[2048,128]{1,0:T(8,128)(2,1)S(1)} %copy-done.3, ...), custom_call_target="tpu_custom_call" | custom-call | flops 1342177280 | bytes 3145728 | tf_op jit(solution)/shard_map/attention/pallas_call | solution.py:312
  100.4 3.8 %collective-permute-done.28.refs_2_.n3 = bf16[128,2560]{1,0:T(8,128)(2,1)S(1)} collective-permute-done((bf16[128,2560]{1,0:T(8,128)(2,1)S(1)}, bf16[128,2560]{1,0:T(8,128)(2,1)S(1)}, u32[]{:S(2)}, u32[]{:S(2)}) %collective-permute-start.28) | collective-permute-done | bytes 655392 | tf_op jit(solution)/shard_map/ppermute | solution.py:154
  104.3 2.7 %collective-permute-start.29 = (bf16[384,2560]{1,0:T(8,128)(2,1)S(1)}, bf16[384,2560]{1,0:T(8,128)(2,1)S(1)}, u32[]{:S(2)}, u32[]{:S(2)}) collective-permute-start(bf16[384,2560]{1,0:T(8,128)(2,1)S(1)} %stack.191), channel_id=1, source_target_pairs={{0,32},{32,0},{1,33},{33,1},{2,34},{34,2},{3,35},{35,3},{4,36},{36... | collective-permute-start | bytes 5898248 | tf_op jit(solution)/shard_map/ppermute | solution.py:62
  107.1 2.6 %collective-permute-start.18 = (bf16[528,128]{1,0:T(8,128)(2,1)S(1)}, bf16[528,128]{1,0:T(8,128)(2,1)S(1)}, u32[]{:S(2)}, u32[]{:S(2)}) collective-permute-start(bf16[528,128]{1,0:T(8,128)(2,1)S(1)} %get-tuple-element.108), channel_id=1, source_target_pairs={{0,32},{32,64},{64,96},{96,128},{128,160},{160,192},{192,224},{224... | collective-permute-start | bytes 405512 | tf_op jit(solution)/shard_map/ppermute | solution.py:58
  110.8 4.6 %collective-permute-start.24 = (bf16[528,128]{1,0:T(8,128)(2,1)S(1)}, bf16[528,128]{1,0:T(8,128)(2,1)S(1)}, u32[]{:S(2)}, u32[]{:S(2)}) collective-permute-start(bf16[528,128]{1,0:T(8,128)(2,1)S(1)} %attention.5), channel_id=1, source_target_pairs={{0,96},{32,128},{64,160},{96,192},{128,224},{160,0},{192,32},{224,... | collective-permute-start | bytes 405512 | tf_op jit(solution)/shard_map/ppermute | solution.py:58
  115.4 5.4 %collective-permute-done.19.refs_2_ = bf16[528,128]{1,0:T(8,128)(2,1)S(1)} collective-permute-done((bf16[528,128]{1,0:T(8,128)(2,1)S(1)}, bf16[528,128]{1,0:T(8,128)(2,1)S(1)}, u32[]{:S(2)}, u32[]{:S(2)}) %collective-permute-start.19) | collective-permute-done | bytes 135200 | tf_op jit(solution)/shard_map/ppermute | solution.py:58
  120.8 5.2 %collective-permute-done.24.refs_3_ = bf16[528,128]{1,0:T(8,128)(2,1)S(1)} collective-permute-done((bf16[528,128]{1,0:T(8,128)(2,1)S(1)}, bf16[528,128]{1,0:T(8,128)(2,1)S(1)}, u32[]{:S(2)}, u32[]{:S(2)}) %collective-permute-start.24) | collective-permute-done | bytes 135200 | tf_op jit(solution)/shard_map/ppermute | solution.py:58
  126.6 1.6 collective-permute-start.26
  128.3 1.6 collective-permute-start.27
  130.7 2.0 %collective-permute-done.27.t3 = bf16[128,128]{1,0:T(8,128)(2,1)S(1)} collective-permute-done((bf16[128,128]{1,0:T(8,128)(2,1)S(1)}, bf16[128,128]{1,0:T(8,128)(2,1)S(1)}, u32[]{:S(2)}, u32[]{:S(2)}) %collective-permute-start.27) | collective-permute-done | bytes 32800 | tf_op jit(solution)/shard_map/ppermute | solution.py:674
  132.7 1.4 out_project.1
  134.2 9.7 %collective-permute-done.30.got_ref = bf16[64,5120]{1,0:T(8,128)(2,1)S(1)} collective-permute-done((bf16[64,5120]{1,0:T(8,128)(2,1)S(1)}, bf16[64,5120]{1,0:T(8,128)(2,1)S(1)}, u32[]{:S(2)}, u32[]{:S(2)}) %collective-permute-start.30) | collective-permute-done | bytes 655392 | tf_op jit(solution)/shard_map/ppermute | solution.py:54
  144.2 4.9 %collective-permute-start.32 = (bf16[512,256]{1,0:T(8,128)(2,1)S(1)}, bf16[512,256]{1,0:T(8,128)(2,1)S(1)}, u32[]{:S(2)}, u32[]{:S(2)}) collective-permute-start(bf16[512,256]{1,0:T(8,128)(2,1)S(1)} %relay.3), channel_id=1, source_target_pairs={{0,128},{32,160},{64,96},{224,192},{1,129},{33,161},{65,97},{225,1... | collective-permute-start | bytes 786440 | tf_op jit(solution)/shard_map/ppermute | solution.py:678
  149.1 2.0 %collective-permute-start.34 = (bf16[32,5120]{1,0:T(8,128)(2,1)S(1)}, bf16[32,5120]{1,0:T(8,128)(2,1)S(1)}, u32[]{:S(2)}, u32[]{:S(2)}) collective-permute-start(bf16[32,5120]{1,0:T(8,128)(2,1)S(1)} %copy-done.6), channel_id=1, source_target_pairs={{0,224},{32,0},{64,32},{96,64},{128,96},{160,128},{192,160},{224,1... | collective-permute-start | bytes 983048 | tf_op jit(solution)/shard_map/ppermute | solution.py:58
  151.1 2.0 %collective-permute-done.32.second_ref = bf16[512,256]{1,0:T(8,128)(2,1)S(1)} collective-permute-done((bf16[512,256]{1,0:T(8,128)(2,1)S(1)}, bf16[512,256]{1,0:T(8,128)(2,1)S(1)}, u32[]{:S(2)}, u32[]{:S(2)}) %collective-permute-start.32) | collective-permute-done | bytes 262176 | tf_op jit(solution)/shard_map/ppermute | solution.py:678
  153.9 7.1 %collective-permute-done.33.got_ref = bf16[16,5120]{1,0:T(8,128)(2,1)S(1)} collective-permute-done((bf16[16,5120]{1,0:T(8,128)(2,1)S(1)}, bf16[16,5120]{1,0:T(8,128)(2,1)S(1)}, u32[]{:S(2)}, u32[]{:S(2)}) %collective-permute-start.33) | collective-permute-done | bytes 163872 | tf_op jit(solution)/shard_map/ppermute | solution.py:54
  161.9 1.3 collective-permute-start.36
  163.8 1.7 insert_rows.1
  165.6 5.5 %collective-permute-done.36 = bf16[16,5120]{1,0:T(8,128)(2,1)S(1)} collective-permute-done((bf16[16,5120]{1,0:T(8,128)(2,1)S(1)}, bf16[16,5120]{1,0:T(8,128)(2,1)S(1)}, u32[]{:S(2)}, u32[]{:S(2)}) %collective-permute-start.36) | collective-permute-done | bytes 163872 | tf_op jit(solution)/shard_map/ppermute | solution.py:693
  171.7 1.3 collective-permute-start.38
  (84 shorter events, 17.1 us)
Async XLA Ops:
  0.6 1.4 copy-start
  3.2 0.9 copy-start.4
  4.5 0.7 copy-start.5
  5.2 5.9 %collective-permute-start = (bf16[16,5120]{1,0:T(8,128)(2,1)S(1)}, bf16[16,5120]{1,0:T(8,128)(2,1)}, u32[]{:S(2)}, u32[]{:S(2)}) collective-permute-start(bf16[16,5120]{1,0:T(8,128)(2,1)S(1)} %get-tuple-element.73.refs_0_), channel_id=1, source_target_pairs={{0,4},{4,0},{1,5},{5,1},{2,6},{6,2},{3,7},{7,3},{8,12},{12,8},{9,1... | collective-permute-start | bytes 491528 | tf_op jit(solution)/shard_map/ppermute | solution.py:39
  9.7 22.5 %copy-start.2 = (bf16[2048,128]{1,0:T(8,128)(2,1)S(1)}, bf16[2048,128]{1,0:T(8,128)(2,1)}, u32[]{:S(2)}) copy-start(bf16[2048,128]{1,0:T(8,128)(2,1)} %k_ref.1) | copy-start | bytes 1572868
  9.7 22.5 %copy-start.3 = (bf16[2048,128]{1,0:T(8,128)(2,1)S(1)}, bf16[2048,128]{1,0:T(8,128)(2,1)}, u32[]{:S(2)}) copy-start(bf16[2048,128]{1,0:T(8,128)(2,1)} %v_ref.1) | copy-start | bytes 1572868
  12.1 6.0 %collective-permute-start.1 = (bf16[32,2560]{1,0:T(8,128)(2,1)S(1)}, bf16[32,2560]{1,0:T(8,128)(2,1)S(1)}, u32[]{:S(2)}, u32[]{:S(2)}) collective-permute-start(bf16[32,2560]{1,0:T(8,128)(2,1)S(1)} %get-tuple-element.87.refs_0_), channel_id=1, source_target_pairs={{0,8},{8,16},{16,24},{24,0},{1,9},{9,17},{17,25},{25,1},{2,10},{10... | collective-permute-start | bytes 491528 | tf_op jit(solution)/shard_map/ppermute | solution.py:158
  13.8 4.2 %collective-permute-start.2 = (bf16[32,2560]{1,0:T(8,128)(2,1)S(1)}, bf16[32,2560]{1,0:T(8,128)(2,1)S(1)}, u32[]{:S(2)}, u32[]{:S(2)}) collective-permute-start(bf16[32,2560]{1,0:T(8,128)(2,1)S(1)} %get-tuple-element.87.refs_0_), channel_id=1, source_target_pairs={{0,24},{8,0},{16,8},{24,16},{1,25},{9,1},{17,9},{25,17},{2,26},{10... | collective-permute-start | bytes 491528 | tf_op jit(solution)/shard_map/ppermute | solution.py:159
  15.2 5.8 %collective-permute-start.4 = (bf16[32,2560]{1,0:T(8,128)(2,1)S(1)}, bf16[32,2560]{1,0:T(8,128)(2,1)S(1)}, u32[]{:S(2)}, u32[]{:S(2)}) collective-permute-start(bf16[32,2560]{1,0:T(8,128)(2,1)S(1)} %get-tuple-element.88.refs_4_), channel_id=1, source_target_pairs={{0,1},{1,2},{2,3},{3,0},{4,5},{5,6},{6,7},{7,4},{8,9},{9,10},{10,1... | collective-permute-start | bytes 491528 | tf_op jit(solution)/shard_map/ppermute | solution.py:158
  16.6 4.4 %collective-permute-start.5 = (bf16[32,2560]{1,0:T(8,128)(2,1)S(1)}, bf16[32,2560]{1,0:T(8,128)(2,1)S(1)}, u32[]{:S(2)}, u32[]{:S(2)}) collective-permute-start(bf16[32,2560]{1,0:T(8,128)(2,1)S(1)} %get-tuple-element.88.refs_4_), channel_id=1, source_target_pairs={{0,3},{1,0},{2,1},{3,2},{4,7},{5,4},{6,5},{7,6},{8,11},{9,8},{10,9... | collective-permute-start | bytes 491528 | tf_op jit(solution)/shard_map/ppermute | solution.py:159
  18.1 5.6 %collective-permute-start.3 = (bf16[32,2560]{1,0:T(8,128)(2,1)S(1)}, bf16[32,2560]{1,0:T(8,128)(2,1)S(1)}, u32[]{:S(2)}, u32[]{:S(2)}) collective-permute-start(bf16[32,2560]{1,0:T(8,128)(2,1)S(1)} %pick.5), channel_id=1, source_target_pairs={{0,8},{8,16},{16,24},{24,0},{32,56},{40,32},{48,40},{56,48},{1,9},... | collective-permute-start | bytes 491528 | tf_op jit(solution)/shard_map/ppermute | solution.py:154
  21.0 4.8 %collective-permute-start.6 = (bf16[32,2560]{1,0:T(8,128)(2,1)S(1)}, bf16[32,2560]{1,0:T(8,128)(2,1)S(1)}, u32[]{:S(2)}, u32[]{:S(2)}) collective-permute-start(bf16[32,2560]{1,0:T(8,128)(2,1)S(1)} %pick.6), channel_id=1, source_target_pairs={{0,1},{1,2},{2,3},{3,0},{32,35},{33,32},{34,33},{35,34},{4,5},{5,6... | collective-permute-start | bytes 491528 | tf_op jit(solution)/shard_map/ppermute | solution.py:154
  26.0 13.8 %collective-permute-start.7 = (bf16[128,2560]{1,0:T(8,128)(2,1)S(1)}, bf16[128,2560]{1,0:T(8,128)(2,1)S(1)}, u32[]{:S(2)}, u32[]{:S(2)}) collective-permute-start(bf16[128,2560]{1,0:T(8,128)(2,1)S(1)} %get-tuple-element.91.refs_1_), channel_id=1, source_target_pairs={{0,1},{1,2},{2,3},{3,0},{4,5},{5,6},{6,7},{7,4},{8,9},{9,10},{10,1... | collective-permute-start | bytes 1966088 | tf_op jit(solution)/shard_map/ppermute | solution.py:158
  27.1 12.7 %collective-permute-start.9 = (bf16[128,2560]{1,0:T(8,128)(2,1)S(1)}, bf16[128,2560]{1,0:T(8,128)(2,1)S(1)}, u32[]{:S(2)}, u32[]{:S(2)}) collective-permute-start(bf16[128,2560]{1,0:T(8,128)(2,1)S(1)} %get-tuple-element.91.refs_1_), channel_id=1, source_target_pairs={{0,3},{1,0},{2,1},{3,2},{4,7},{5,4},{6,5},{7,6},{8,11},{9,8},{10,9... | collective-permute-start | bytes 1966088 | tf_op jit(solution)/shard_map/ppermute | solution.py:159
  29.5 13.1 %collective-permute-start.8 = (bf16[128,2560]{1,0:T(8,128)(2,1)S(1)}, bf16[128,2560]{1,0:T(8,128)(2,1)S(1)}, u32[]{:S(2)}, u32[]{:S(2)}) collective-permute-start(bf16[128,2560]{1,0:T(8,128)(2,1)S(1)} %get-tuple-element.92.refs_2_), channel_id=1, source_target_pairs={{0,8},{8,16},{16,24},{24,0},{1,9},{9,17},{17,25},{25,1},{2,10},{10... | collective-permute-start | bytes 1966088 | tf_op jit(solution)/shard_map/ppermute | solution.py:158
  29.5 13.1 %collective-permute-start.10 = (bf16[128,2560]{1,0:T(8,128)(2,1)S(1)}, bf16[128,2560]{1,0:T(8,128)(2,1)S(1)}, u32[]{:S(2)}, u32[]{:S(2)}) collective-permute-start(bf16[128,2560]{1,0:T(8,128)(2,1)S(1)} %get-tuple-element.92.refs_2_), channel_id=1, source_target_pairs={{0,24},{8,0},{16,8},{24,16},{1,25},{9,1},{17,9},{25,17},{2,26},{10... | collective-permute-start | bytes 1966088 | tf_op jit(solution)/shard_map/ppermute | solution.py:159
  32.4 12.0 %copy-start.1 = (bf16[3,5120,128]{2,1,0:T(8,128)(2,1)S(1)}, bf16[3,5120,128]{2,1,0:T(8,128)(2,1)}, u32[]{:S(2)}) copy-start(bf16[3,5120,128]{2,1,0:T(8,128)(2,1)} %refs_3_.6) | copy-start | bytes 11796484
  32.4 16.7 %collective-permute-start.13 = (bf16[2048,256]{1,0:T(8,128)(2,1)S(1)}, bf16[2048,256]{1,0:T(8,128)(2,1)S(1)}, u32[]{:S(2)}, u32[]{:S(2)}) collective-permute-start(bf16[2048,256]{1,0:T(8,128)(2,1)S(1)} %beside.1), channel_id=1, source_target_pairs={{0,32},{32,0},{1,33},{33,1},{2,34},{34,2},{3,35},{35,3},{4,36},{36... | collective-permute-start | bytes 3145736 | tf_op jit(solution)/shard_map/ppermute | solution.py:62
  39.8 11.3 %collective-permute-start.11 = (bf16[128,2560]{1,0:T(8,128)(2,1)S(1)}, bf16[128,2560]{1,0:T(8,128)(2,1)S(1)}, u32[]{:S(2)}, u32[]{:S(2)}) collective-permute-start(bf16[128,2560]{1,0:T(8,128)(2,1)S(1)} %pick.7), channel_id=1, source_target_pairs={{0,1},{1,2},{2,3},{3,0},{32,35},{33,32},{34,33},{35,34},{4,5},{5,6... | collective-permute-start | bytes 1966088 | tf_op jit(solution)/shard_map/ppermute | solution.py:154
  42.6 11.1 %collective-permute-start.12 = (bf16[128,2560]{1,0:T(8,128)(2,1)S(1)}, bf16[128,2560]{1,0:T(8,128)(2,1)S(1)}, u32[]{:S(2)}, u32[]{:S(2)}) collective-permute-start(bf16[128,2560]{1,0:T(8,128)(2,1)S(1)} %pick.8), channel_id=1, source_target_pairs={{0,8},{8,16},{16,24},{24,0},{32,56},{40,32},{48,40},{56,48},{1,9},... | collective-permute-start | bytes 1966088 | tf_op jit(solution)/shard_map/ppermute | solution.py:154
  55.6 13.2 %collective-permute-start.14 = (bf16[512,256]{1,0:T(8,128)(2,1)S(1)}, bf16[512,256]{1,0:T(8,128)(2,1)S(1)}, u32[]{:S(2)}, u32[]{:S(2)}) collective-permute-start(bf16[512,256]{1,0:T(8,128)(2,1)S(1)} %get-tuple-element.101.refs_5_.refs_6_.own_ref.got_ref), channel_id=1, source_target_pairs={{0,32},{32,0},{1,33},{33,1},{2,34},{34,2},{3,35},{35,3},{4,36},{36... | collective-permute-start | bytes 786440 | tf_op jit(solution)/shard_map/ppermute | solution.py:62
  63.5 10.8 %collective-permute-start.15 = (bf16[512,128]{1,0:T(8,128)(2,1)S(1)}, bf16[512,128]{1,0:T(8,128)(2,1)S(1)}, u32[]{:S(2)}, u32[]{:S(2)}) collective-permute-start(bf16[512,128]{1,0:T(8,128)(2,1)S(1)} %get-tuple-element.99.refs_1_), channel_id=1, source_target_pairs={{0,192},{32,224},{64,0},{96,32},{128,64},{160,96},{192,128},{224,1... | collective-permute-start | bytes 393224 | tf_op jit(solution)/shard_map/ppermute | solution.py:58
  68.8 7.5 %collective-permute-start.16 = (bf16[512,128]{1,0:T(8,128)(2,1)S(1)}, bf16[512,128]{1,0:T(8,128)(2,1)S(1)}, u32[]{:S(2)}, u32[]{:S(2)}) collective-permute-start(bf16[512,128]{1,0:T(8,128)(2,1)S(1)} %get-tuple-element.99.refs_1_), channel_id=1, source_target_pairs={{0,64},{32,96},{64,128},{96,160},{128,192},{160,224},{192,0},{224,... | collective-permute-start | bytes 393224 | tf_op jit(solution)/shard_map/ppermute | solution.py:58
  76.3 17.8 %collective-permute-start.21 = (bf16[128,2560]{1,0:T(8,128)(2,1)S(1)}, bf16[128,2560]{1,0:T(8,128)(2,1)S(1)}, u32[]{:S(2)}, u32[]{:S(2)}) collective-permute-start(bf16[128,2560]{1,0:T(8,128)(2,1)S(1)} %get-tuple-element.111.n0), channel_id=1, source_target_pairs={{0,8},{8,0},{16,24},{24,16},{1,9},{9,1},{17,25},{25,17},{2,10},{10... | collective-permute-start | bytes 1966088 | tf_op jit(solution)/shard_map/ppermute | solution.py:39
  76.3 17.8 %collective-permute-start.22 = (bf16[128,2560]{1,0:T(8,128)(2,1)S(1)}, bf16[128,2560]{1,0:T(8,128)(2,1)S(1)}, u32[]{:S(2)}, u32[]{:S(2)}) collective-permute-start(bf16[128,2560]{1,0:T(8,128)(2,1)S(1)} %get-tuple-element.111.n0), channel_id=1, source_target_pairs={{0,24},{8,16},{16,8},{24,0},{1,25},{9,17},{17,9},{25,1},{2,26},{10... | collective-permute-start | bytes 1966088 | tf_op jit(solution)/shard_map/ppermute | solution.py:39
  78.1 16.0 %collective-permute-start.23 = (bf16[512,256]{1,0:T(8,128)(2,1)S(1)}, bf16[512,256]{1,0:T(8,128)(2,1)S(1)}, u32[]{:S(2)}, u32[]{:S(2)}) collective-permute-start(bf16[512,256]{1,0:T(8,128)(2,1)S(1)} %relay.2), channel_id=1, source_target_pairs={{0,64},{32,224},{1,65},{33,225},{2,66},{34,226},{3,67},{35,227},{4... | collective-permute-start | bytes 786440 | tf_op jit(solution)/shard_map/ppermute | solution.py:655
  82.4 11.4 %collective-permute-start.20 = (bf16[512,128]{1,0:T(8,128)(2,1)S(1)}, bf16[512,128]{1,0:T(8,128)(2,1)S(1)}, u32[]{:S(2)}, u32[]{:S(2)}) collective-permute-start(bf16[512,128]{1,0:T(8,128)(2,1)S(1)} %get-tuple-element.99.refs_1_), channel_id=1, source_target_pairs={{0,128},{32,160},{64,192},{96,224},{128,0},{160,32},{192,64},{224,... | collective-permute-start | bytes 393224 | tf_op jit(solution)/shard_map/ppermute | solution.py:58
  94.2 10.0 %collective-permute-start.28 = (bf16[128,2560]{1,0:T(8,128)(2,1)S(1)}, bf16[128,2560]{1,0:T(8,128)(2,1)S(1)}, u32[]{:S(2)}, u32[]{:S(2)}) collective-permute-start(bf16[128,2560]{1,0:T(8,128)(2,1)S(1)} %pick.9), channel_id=1, source_target_pairs={{0,24},{8,16},{16,8},{24,0},{32,40},{40,32},{48,56},{56,48},{1,25}... | collective-permute-start | bytes 1966088 | tf_op jit(solution)/shard_map/ppermute | solution.py:154
  104.3 28.3 %collective-permute-start.29 = (bf16[384,2560]{1,0:T(8,128)(2,1)S(1)}, bf16[384,2560]{1,0:T(8,128)(2,1)S(1)}, u32[]{:S(2)}, u32[]{:S(2)}) collective-permute-start(bf16[384,2560]{1,0:T(8,128)(2,1)S(1)} %stack.191), channel_id=1, source_target_pairs={{0,32},{32,0},{1,33},{33,1},{2,34},{34,2},{3,35},{35,3},{4,36},{36... | collective-permute-start | bytes 5898248 | tf_op jit(solution)/shard_map/ppermute | solution.py:62
  107.0 8.3 %collective-permute-start.17 = (bf16[528,128]{1,0:T(8,128)(2,1)S(1)}, bf16[528,128]{1,0:T(8,128)(2,1)S(1)}, u32[]{:S(2)}, u32[]{:S(2)}) collective-permute-start(bf16[528,128]{1,0:T(8,128)(2,1)S(1)} %attention.3), channel_id=1, source_target_pairs={{0,224},{32,0},{64,32},{96,64},{128,96},{160,128},{192,160},{224,1... | collective-permute-start | bytes 405512 | tf_op jit(solution)/shard_map/ppermute | solution.py:58
  107.1 8.2 %collective-permute-start.18 = (bf16[528,128]{1,0:T(8,128)(2,1)S(1)}, bf16[528,128]{1,0:T(8,128)(2,1)S(1)}, u32[]{:S(2)}, u32[]{:S(2)}) collective-permute-start(bf16[528,128]{1,0:T(8,128)(2,1)S(1)} %get-tuple-element.108), channel_id=1, source_target_pairs={{0,32},{32,64},{64,96},{96,128},{128,160},{160,192},{192,224},{224... | collective-permute-start | bytes 405512 | tf_op jit(solution)/shard_map/ppermute | solution.py:58
  109.7 11.1 %collective-permute-start.19 = (bf16[528,128]{1,0:T(8,128)(2,1)S(1)}, bf16[528,128]{1,0:T(8,128)(2,1)S(1)}, u32[]{:S(2)}, u32[]{:S(2)}) collective-permute-start(bf16[528,128]{1,0:T(8,128)(2,1)S(1)} %get-tuple-element.109), channel_id=1, source_target_pairs={{0,160},{32,192},{64,224},{96,0},{128,32},{160,64},{192,96},{224,1... | collective-permute-start | bytes 405512 | tf_op jit(solution)/shard_map/ppermute | solution.py:58
  110.8 15.2 %collective-permute-start.24 = (bf16[528,128]{1,0:T(8,128)(2,1)S(1)}, bf16[528,128]{1,0:T(8,128)(2,1)S(1)}, u32[]{:S(2)}, u32[]{:S(2)}) collective-permute-start(bf16[528,128]{1,0:T(8,128)(2,1)S(1)} %attention.5), channel_id=1, source_target_pairs={{0,96},{32,128},{64,160},{96,192},{128,224},{160,0},{192,32},{224,... | collective-permute-start | bytes 405512 | tf_op jit(solution)/shard_map/ppermute | solution.py:58
  126.5 3.3 %collective-permute-start.25 = (bf16[128,128]{1,0:T(8,128)(2,1)S(1)}, bf16[128,128]{1,0:T(8,128)(2,1)S(1)}, u32[]{:S(2)}, u32[]{:S(2)}) collective-permute-start(bf16[128,128]{1,0:T(8,128)(2,1)S(1)} %get-tuple-element.148), channel_id=1, source_target_pairs={{0,8},{8,0},{16,24},{24,16},{1,9},{9,1},{17,25},{25,17},{2,10},{10... | collective-permute-start | bytes 98312 | tf_op jit(solution)/shard_map/ppermute | solution.py:39
  126.6 4.1 %collective-permute-start.26 = (bf16[128,128]{1,0:T(8,128)(2,1)S(1)}, bf16[128,128]{1,0:T(8,128)(2,1)S(1)}, u32[]{:S(2)}, u32[]{:S(2)}) collective-permute-start(bf16[128,128]{1,0:T(8,128)(2,1)S(1)} %get-tuple-element.147), channel_id=1, source_target_pairs={{0,24},{8,16},{16,8},{24,0},{1,25},{9,17},{17,9},{25,1},{2,26},{10... | collective-permute-start | bytes 98312 | tf_op jit(solution)/shard_map/ppermute | solution.py:39
  128.3 4.4 %collective-permute-start.27 = (bf16[128,128]{1,0:T(8,128)(2,1)S(1)}, bf16[128,128]{1,0:T(8,128)(2,1)S(1)}, u32[]{:S(2)}, u32[]{:S(2)}) collective-permute-start(bf16[128,128]{1,0:T(8,128)(2,1)S(1)} %get-tuple-element.146), channel_id=1, source_target_pairs={{0,16},{8,24},{16,0},{24,8},{1,17},{9,25},{17,1},{25,9},{2,18},{10... | collective-permute-start | bytes 98312 | tf_op jit(solution)/shard_map/ppermute | solution.py:674
  134.1 15.1 %copy-start.6 = (bf16[32,5120]{1,0:T(8,128)(2,1)S(1)}, bf16[32,5120]{1,0:T(8,128)(2,1)}, u32[]{:S(2)}) copy-start(bf16[32,5120]{1,0:T(8,128)(2,1)} %copy-done.5) | copy-start | bytes 983044
  134.1 9.8 %collective-permute-start.30 = (bf16[64,5120]{1,0:T(8,128)(2,1)S(1)}, bf16[64,5120]{1,0:T(8,128)(2,1)S(1)}, u32[]{:S(2)}, u32[]{:S(2)}) collective-permute-start(bf16[64,5120]{1,0:T(8,128)(2,1)S(1)} %get-tuple-element.120), channel_id=1, source_target_pairs={{0,4},{1,5},{2,6},{3,7},{4,0},{5,1},{6,2},{7,3},{8,12},{9,13},{10,... | collective-permute-start | bytes 1966088 | tf_op jit(solution)/shard_map/ppermute | solution.py:54
  144.1 9.1 %collective-permute-start.31 = (bf16[32,5120]{1,0:T(8,128)(2,1)S(1)}, bf16[32,5120]{1,0:T(8,128)(2,1)S(1)}, u32[]{:S(2)}, u32[]{:S(2)}) collective-permute-start(bf16[32,5120]{1,0:T(8,128)(2,1)S(1)} %get-tuple-element.122), channel_id=1, source_target_pairs={{0,1},{1,0},{2,3},{3,2},{4,5},{5,4},{6,7},{7,6},{8,9},{9,8},{10,11... | collective-permute-start | bytes 983048 | tf_op jit(solution)/shard_map/ppermute | solution.py:54
  144.2 8.9 %collective-permute-start.32 = (bf16[512,256]{1,0:T(8,128)(2,1)S(1)}, bf16[512,256]{1,0:T(8,128)(2,1)S(1)}, u32[]{:S(2)}, u32[]{:S(2)}) collective-permute-start(bf16[512,256]{1,0:T(8,128)(2,1)S(1)} %relay.3), channel_id=1, source_target_pairs={{0,128},{32,160},{64,96},{224,192},{1,129},{33,161},{65,97},{225,1... | collective-permute-start | bytes 786440 | tf_op jit(solution)/shard_map/ppermute | solution.py:678
  149.1 11.9 %collective-permute-start.34 = (bf16[32,5120]{1,0:T(8,128)(2,1)S(1)}, bf16[32,5120]{1,0:T(8,128)(2,1)S(1)}, u32[]{:S(2)}, u32[]{:S(2)}) collective-permute-start(bf16[32,5120]{1,0:T(8,128)(2,1)S(1)} %copy-done.6), channel_id=1, source_target_pairs={{0,224},{32,0},{64,32},{96,64},{128,96},{160,128},{192,160},{224,1... | collective-permute-start | bytes 983048 | tf_op jit(solution)/shard_map/ppermute | solution.py:58
  153.2 7.8 %collective-permute-start.33 = (bf16[16,5120]{1,0:T(8,128)(2,1)S(1)}, bf16[16,5120]{1,0:T(8,128)(2,1)S(1)}, u32[]{:S(2)}, u32[]{:S(2)}) collective-permute-start(bf16[16,5120]{1,0:T(8,128)(2,1)S(1)} %get-tuple-element.127), channel_id=1, source_target_pairs={{0,3},{1,2},{2,1},{3,0},{4,7},{5,6},{6,5},{7,4},{8,11},{9,10},{10,... | collective-permute-start | bytes 491528 | tf_op jit(solution)/shard_map/ppermute | solution.py:54
  161.2 4.4 %collective-permute-start.35 = (bf16[16,5120]{1,0:T(8,128)(2,1)S(1)}, bf16[16,5120]{1,0:T(8,128)(2,1)S(1)}, u32[]{:S(2)}, u32[]{:S(2)}) collective-permute-start(bf16[16,5120]{1,0:T(8,128)(2,1)S(1)} %finish.1), channel_id=1, source_target_pairs={{224,96},{225,97},{226,98},{227,99},{228,100},{229,101},{230,102},... | collective-permute-start | bytes 491528 | tf_op jit(solution)/shard_map/ppermute | solution.py:693
  161.9 9.2 %collective-permute-start.36 = (bf16[16,5120]{1,0:T(8,128)(2,1)S(1)}, bf16[16,5120]{1,0:T(8,128)(2,1)S(1)}, u32[]{:S(2)}, u32[]{:S(2)}) collective-permute-start(bf16[16,5120]{1,0:T(8,128)(2,1)S(1)} %finish.1), channel_id=1, source_target_pairs={{224,32},{225,33},{226,34},{227,35},{228,36},{229,37},{230,38},{23... | collective-permute-start | bytes 491528 | tf_op jit(solution)/shard_map/ppermute | solution.py:693
  163.2 7.9 %collective-permute-start.37 = (bf16[16,5120]{1,0:T(8,128)(2,1)S(1)}, bf16[16,5120]{1,0:T(8,128)(2,1)S(1)}, u32[]{:S(2)}, u32[]{:S(2)}) collective-permute-start(bf16[16,5120]{1,0:T(8,128)(2,1)S(1)} %finish.1), channel_id=1, source_target_pairs={{224,160},{225,161},{226,162},{227,163},{228,164},{229,165},{230,1... | collective-permute-start | bytes 491528 | tf_op jit(solution)/shard_map/ppermute | solution.py:693
  171.7 2.3 %collective-permute-start.38 = (bf16[16,5120]{1,0:T(8,128)(2,1)S(1)}, bf16[16,5120]{1,0:T(8,128)(2,1)S(1)}, u32[]{:S(2)}, u32[]{:S(2)}) collective-permute-start(bf16[16,5120]{1,0:T(8,128)(2,1)S(1)} %get-tuple-element.144), channel_id=1, source_target_pairs={{32,0},{33,1},{34,2},{35,3},{36,4},{37,5},{38,6},{39,7},{40,8},{41... | collective-permute-start | bytes 491528 | tf_op jit(solution)/shard_map/ppermute | solution.py:699
where the time goes:
time: 175 us
  starting transfers between devices  76.3 us (44%)
  waiting for transfers between devices  55.9 us (32%)
  Pallas kernels  32.5 us (19%)
  local copies, waits for them, and re-layouts  4.57 us (3%)
  between operations  3.2 us (2%)
  other arithmetic  2.27 us (1%)
    pallas_call x3, Pallas kernels, attention(): pl.pallas_call(lambda *refs: attention_body(count, *refs), in_specs=[pl.B...  19.6 us
    ppermute x3, waiting for transfers between devices, across_each(): return lax.ppermute(block, ('core', 'x', 'zl', 'y'), pairs)  16.9 us
    ppermute x3, starting transfers between devices, other_core(): return lax.ppermute(block, 'core', [(0, 1), (1, 0)])  16.6 us
    ppermute x8, starting transfers between devices, frame_shift(): lax.ppermute(block, FRAME, [(i, (i + distance) % 8) for i in range(8)])  15.7 us
    ppermute x8, waiting for transfers between devices, frame_shift(): lax.ppermute(block, FRAME, [(i, (i + distance) % 8) for i in range(8)])  14.9 us
    ppermute x5, starting transfers between devices, by_core(): return lax.ppermute(block, ('core', axis), pairs)  10.8 us
    ppermute x5, waiting for transfers between devices, by_core(): return lax.ppermute(block, ('core', axis), pairs)  10.8 us
    ppermute x4, starting transfers between devices, ring(): behind = lax.ppermute(block, axis, [(i, (i - 1) % 4) for i in range(4)])  7.93 us
  transfers between devices with their start and end apart: 39, of which 19 were waited for; matrix products, arithmetic and copies ran while one was open for 1% of the time, Pallas kernels for 16%

commit v1 on v0

--- a/solution.py
+++ b/solution.py
@@ -631,7 +631,6 @@
 
     q_up = frame_shift(query, -2)
     q_down = frame_shift(query, 2)
-    q_far = frame_shift(query, 4)
     other_key_value = other_core(key_value)
 
     def attend(table, *queries):
@@ -646,11 +645,11 @@
         )
 
     (part,) = attend(tables[3], query)
-    part, q_up, q_down, w_next, carry = lax.optimization_barrier(
-        (part, q_up, q_down, w_near, carry)
-    )
+    part, query_late, w_next = lax.optimization_barrier((part, query, w_near))
+    q_far = frame_shift(query_late, 4)
     sent = [frame_shift(part, -1)]
-    w_one, w_three = across(w_next, 0), across(w_next, 1)
+    w_one = across(w_next, 0)
+    w_three = across(w_next, 1)
     other_late = after(other_key_value, part)
     root_first = lax.ppermute(
         relay(slots, key_value, other_late, key_value), FRAME, [(0, 2), (1, 7)]
@@ -675,11 +674,8 @@
     together = [attended[0, 0], across(attended[1, 0], 0), across(attended[0, 1], 1), beyond]
     keep, send = out_project(order, together, sides)
     got = across_each(send, REDUCE[0])
-    root_second = lax.ppermute(
-        relay(slots, key_value, other_key_value, after(root_first, send)),
-        FRAME,
-        [(0, 4), (1, 5), (2, 3), (7, 6)],
-    )
+    relayed = relay(slots, key_value, other_key_value, after(root_first, send))
+    root_second = lax.ppermute(relayed, FRAME, [(0, 4), (1, 5), (2, 3), (7, 6)])
     keep, send = add_up(keep, got)
     got = across_each(send, REDUCE[1])
     got, root_second = lax.optimization_barrier((got, root_second))

time: 175 us -> 178 us (1.017)
  starting transfers between devices: 76.3 us -> 81.6 us
  waiting for transfers between devices: 55.9 us -> 52.9 us
    ppermute x8, waiting for transfers between devices: 14.9 us -> 9.43 us  [frame_shift(): lax.ppermute(block, FRAME, [(i, (i + distance) % 8) for i in range(8)])]
    ppermute x1, waiting for transfers between devices: 2.01 us -> 4.17 us  [step(): root_second = lax.ppermute(relayed, FRAME, [(0, 4), (1, 5), (2, 3), (7, 6)])]
    ppermute x8, starting transfers between devices: 15.7 us -> 17.9 us  [frame_shift(): lax.ppermute(block, FRAME, [(i, (i + distance) % 8) for i in range(8)])]
  transfers between devices with their start and end apart: 39 -> 39, of which waited for: 19 -> 17; matrix products, arithmetic and copies ran while one was open for 1% -> 1% of each run, Pallas kernels for 16% -> 13%
where the time goes in v1:
time: 178 us; the launch traced here: 177 us
  starting transfers between devices  81.6 us (46%)
  waiting for transfers between devices  52.9 us (30%)
  Pallas kernels  32.5 us (18%)
  local copies, waits for them, and re-layouts  4.57 us (3%)
  between operations  3.23 us (2%)
  other arithmetic  2.27 us (1%)
    pallas_call x3, Pallas kernels, attention(): pl.pallas_call(lambda *refs: attention_body(count, *refs), in_specs=[pl.B...  19.6 us
    ppermute x3, starting transfers between devices, other_core(): return lax.ppermute(block, 'core', [(0, 1), (1, 0)])  18 us
    ppermute x8, starting transfers between devices, frame_shift(): lax.ppermute(block, FRAME, [(i, (i + distance) % 8) for i in range(8)])  17.9 us
    ppermute x3, waiting for transfers between devices, across_each(): return lax.ppermute(block, ('core', 'x', 'zl', 'y'), pairs)  16.5 us
    ppermute x5, waiting for transfers between devices, by_core(): return lax.ppermute(block, ('core', axis), pairs)  10.9 us
    ppermute x5, starting transfers between devices, by_core(): return lax.ppermute(block, ('core', axis), pairs)  10.7 us
    ppermute x8, waiting for transfers between devices, frame_shift(): lax.ppermute(block, FRAME, [(i, (i + distance) % 8) for i in range(8)])  9.43 us
    ppermute x4, starting transfers between devices, ring(): behind = lax.ppermute(block, axis, [(i, (i - 1) % 4) for i in range(4)])  7.93 us
  transfers between devices with their start and end apart: 39, of which 17 were waited for; matrix products, arithmetic and copies ran while one was open for 1% of the time, Pallas kernels for 13%

profile of v1, /device:TPU:1, one launch (start us, length us, event | category | flops | bytes accessed | tf_op | source)
XLA Modules:
  0.0 177.1 jit_solution(5869013677825412978)
XLA Ops:
  2.1 1.1 constant_dynamic-slice_fusion.3
  5.2 2.5 %collective-permute-start = (bf16[16,5120]{1,0:T(8,128)(2,1)S(1)}, bf16[16,5120]{1,0:T(8,128)(2,1)}, u32[]{:S(2)}, u32[]{:S(2)}) collective-permute-start(bf16[16,5120]{1,0:T(8,128)(2,1)S(1)} %get-tuple-element.71.refs_0_), channel_id=1, source_target_pairs={{0,4},{4,0},{1,5},{5,1},{2,6},{6,2},{3,7},{7,3},{8,12},{12,8},{9,1... | collective-permute-start | bytes 491528 | tf_op jit(solution)/shard_map/ppermute | solution.py:39
  8.4 1.4 constant_dynamic-slice_fusion
  12.1 1.8 collective-permute-start.1
  13.8 1.4 collective-permute-start.2
  15.2 1.4 collective-permute-start.4
  16.6 1.4 collective-permute-start.5
  18.1 2.6 %collective-permute-start.3 = (bf16[32,2560]{1,0:T(8,128)(2,1)S(1)}, bf16[32,2560]{1,0:T(8,128)(2,1)S(1)}, u32[]{:S(2)}, u32[]{:S(2)}) collective-permute-start(bf16[32,2560]{1,0:T(8,128)(2,1)S(1)} %pick.5), channel_id=1, source_target_pairs={{0,8},{8,16},{16,24},{24,0},{32,56},{40,32},{48,40},{56,48},{1,9},... | collective-permute-start | bytes 491528 | tf_op jit(solution)/shard_map/ppermute | solution.py:154
  21.0 2.6 %collective-permute-start.6 = (bf16[32,2560]{1,0:T(8,128)(2,1)S(1)}, bf16[32,2560]{1,0:T(8,128)(2,1)S(1)}, u32[]{:S(2)}, u32[]{:S(2)}) collective-permute-start(bf16[32,2560]{1,0:T(8,128)(2,1)S(1)} %pick.6), channel_id=1, source_target_pairs={{0,1},{1,2},{2,3},{3,0},{32,35},{33,32},{34,33},{35,34},{4,5},{5,6... | collective-permute-start | bytes 491528 | tf_op jit(solution)/shard_map/ppermute | solution.py:154
  23.6 2.3 %collective-permute-done.6.refs_7_ = bf16[32,2560]{1,0:T(8,128)(2,1)S(1)} collective-permute-done((bf16[32,2560]{1,0:T(8,128)(2,1)S(1)}, bf16[32,2560]{1,0:T(8,128)(2,1)S(1)}, u32[]{:S(2)}, u32[]{:S(2)}) %collective-permute-start.6) | collective-permute-done | bytes 163872 | tf_op jit(solution)/shard_map/ppermute | solution.py:154
  26.0 1.1 collective-permute-start.7
  27.1 2.5 %collective-permute-start.9 = (bf16[128,2560]{1,0:T(8,128)(2,1)S(1)}, bf16[128,2560]{1,0:T(8,128)(2,1)S(1)}, u32[]{:S(2)}, u32[]{:S(2)}) collective-permute-start(bf16[128,2560]{1,0:T(8,128)(2,1)S(1)} %get-tuple-element.89.refs_1_), channel_id=1, source_target_pairs={{0,3},{1,0},{2,1},{3,2},{4,7},{5,4},{6,5},{7,6},{8,11},{9,8},{10,9... | collective-permute-start | bytes 1966088 | tf_op jit(solution)/shard_map/ppermute | solution.py:159
  29.5 2.7 %collective-permute-start.10 = (bf16[128,2560]{1,0:T(8,128)(2,1)S(1)}, bf16[128,2560]{1,0:T(8,128)(2,1)S(1)}, u32[]{:S(2)}, u32[]{:S(2)}) collective-permute-start(bf16[128,2560]{1,0:T(8,128)(2,1)S(1)} %get-tuple-element.90.refs_2_), channel_id=1, source_target_pairs={{0,24},{8,0},{16,8},{24,16},{1,25},{9,1},{17,9},{25,17},{2,26},{10... | collective-permute-start | bytes 1966088 | tf_op jit(solution)/shard_map/ppermute | solution.py:159
  32.4 6.0 %collective-permute-start.13 = (bf16[2048,256]{1,0:T(8,128)(2,1)S(1)}, bf16[2048,256]{1,0:T(8,128)(2,1)S(1)}, u32[]{:S(2)}, u32[]{:S(2)}) collective-permute-start(bf16[2048,256]{1,0:T(8,128)(2,1)S(1)} %beside.1), channel_id=1, source_target_pairs={{0,32},{32,0},{1,33},{33,1},{2,34},{34,2},{3,35},{35,3},{4,36},{36... | collective-permute-start | bytes 3145736 | tf_op jit(solution)/shard_map/ppermute | solution.py:62
  38.4 1.4 collective-permute-done.7.refs_1_.first_ref
  39.8 2.7 %collective-permute-start.11 = (bf16[128,2560]{1,0:T(8,128)(2,1)S(1)}, bf16[128,2560]{1,0:T(8,128)(2,1)S(1)}, u32[]{:S(2)}, u32[]{:S(2)}) collective-permute-start(bf16[128,2560]{1,0:T(8,128)(2,1)S(1)} %pick.7), channel_id=1, source_target_pairs={{0,1},{1,2},{2,3},{3,0},{32,35},{33,32},{34,33},{35,34},{4,5},{5,6... | collective-permute-start | bytes 1966088 | tf_op jit(solution)/shard_map/ppermute | solution.py:154
  42.6 1.8 collective-permute-start.12
  44.4 1.8 qkv_add.2.refs_6_
  46.2 2.9 %qkv_add.3.refs_4_ = f32[512,384]{1,0:T(8,128)S(1)} custom-call(s32[32]{0:T(128)S(1)} %stack.176.refs_0_, bf16[128,2560]{1,0:T(8,128)(2,1)S(1)} %collective-permute-done.7.refs_1_.first_ref, bf16[128,2560]{1,0:T(8,128)(2,1)S(1)} %collective-permute-done.8.refs_2_.first_ref, bf16[128,2560]{1,0:T(8,128)(2,1)S(1)} %collective-permute-done.9.refs_3_.second_ref, ...), custom_call_target="tpu_custom_call" | custom-call | flops 1006632960 | bytes 6291456 | tf_op jit(solution)/shard_map/qkv_add/pallas_call | solution.py:205
  49.1 2.0 %collective-permute-done.11.refs_1_ = bf16[128,2560]{1,0:T(8,128)(2,1)S(1)} collective-permute-done((bf16[128,2560]{1,0:T(8,128)(2,1)S(1)}, bf16[128,2560]{1,0:T(8,128)(2,1)S(1)}, u32[]{:S(2)}, u32[]{:S(2)}) %collective-permute-start.11) | collective-permute-done | bytes 655392 | tf_op jit(solution)/shard_map/ppermute | solution.py:154
  51.1 2.7 %collective-permute-done.12.refs_2_ = bf16[128,2560]{1,0:T(8,128)(2,1)S(1)} collective-permute-done((bf16[128,2560]{1,0:T(8,128)(2,1)S(1)}, bf16[128,2560]{1,0:T(8,128)(2,1)S(1)}, u32[]{:S(2)}, u32[]{:S(2)}) %collective-permute-start.12) | collective-permute-done | bytes 655392 | tf_op jit(solution)/shard_map/ppermute | solution.py:154
  53.8 1.8 %qkv_last.1 = (bf16[512,128]{1,0:T(8,128)(2,1)S(1)}, bf16[512,256]{1,0:T(8,128)(2,1)S(1)}) custom-call(s32[16]{0:T(128)S(1)} %stack.177.refs_0_, bf16[128,2560]{1,0:T(8,128)(2,1)S(1)} %collective-permute-done.11.refs_1_, bf16[128,2560]{1,0:T(8,128)(2,1)S(1)} %collective-permute-done.12.refs_2_, bf16[3,5120,128]{2,1,0:T(8,128)(2,1)S(1)} %copy-done.1, ...), custom_call_target="tpu_custom_call" | custom-call | flops 503316480 | bytes 6291456 | tf_op jit(solution)/shard_map/qkv_last/pallas_call | solution.py:205
  55.6 7.9 %collective-permute-start.14 = (bf16[512,256]{1,0:T(8,128)(2,1)S(1)}, bf16[512,256]{1,0:T(8,128)(2,1)S(1)}, u32[]{:S(2)}, u32[]{:S(2)}) collective-permute-start(bf16[512,256]{1,0:T(8,128)(2,1)S(1)} %get-tuple-element.99.refs_5_.refs_6_.own_ref.got_ref), channel_id=1, source_target_pairs={{0,32},{32,0},{1,33},{33,1},{2,34},{34,2},{3,35},{35,3},{4,36},{36... | collective-permute-start | bytes 786440 | tf_op jit(solution)/shard_map/ppermute | solution.py:62
  63.5 1.2 collective-permute-done.14.refs_6_.refs_7_.other_ref
  64.6 5.0 %attention.3 = bf16[528,128]{1,0:T(8,128)(2,1)S(1)} custom-call(s32[4]{0:T(128)S(1)} %get-tuple-element.81.refs_0_, bf16[512,128]{1,0:T(8,128)(2,1)S(1)} %get-tuple-element.106.refs_1_, bf16[2048,128]{1,0:T(8,128)(2,1)S(1)} %copy-done.2, bf16[2048,128]{1,0:T(8,128)(2,1)S(1)} %copy-done.3, bf16[2048,256]{1,0:T(8,128)(2,1)S(1)} %collective-permute-done.13.refs_4_.refs_5_, ...), custom_call_target="tpu_custom_call" | custom-call | flops 1342177280 | bytes 3145728 | tf_op jit(solution)/shard_map/attention/pallas_call | solution.py:312
  69.8 1.8 %collective-permute-start.22 = (bf16[128,2560]{1,0:T(8,128)(2,1)S(1)}, bf16[128,2560]{1,0:T(8,128)(2,1)S(1)}, u32[]{:S(2)}, u32[]{:S(2)}) collective-permute-start(bf16[128,2560]{1,0:T(8,128)(2,1)S(1)} %get-tuple-element.107.n0), channel_id=1, source_target_pairs={{0,24},{8,16},{16,8},{24,0},{1,25},{9,17},{17,9},{25,1},{2,26},{10... | collective-permute-start | bytes 1966088 | tf_op jit(solution)/shard_map/ppermute | solution.py:39
  71.6 5.3 %collective-permute-start.16 = (bf16[512,128]{1,0:T(8,128)(2,1)S(1)}, bf16[512,128]{1,0:T(8,128)(2,1)S(1)}, u32[]{:S(2)}, u32[]{:S(2)}) collective-permute-start(bf16[512,128]{1,0:T(8,128)(2,1)S(1)} %get-tuple-element.106.refs_1_), channel_id=1, source_target_pairs={{0,192},{32,224},{64,0},{96,32},{128,64},{160,96},{192,128},{224,1... | collective-permute-start | bytes 393224 | tf_op jit(solution)/shard_map/ppermute | solution.py:58
  77.0 5.5 %collective-permute-start.23 = (bf16[512,256]{1,0:T(8,128)(2,1)S(1)}, bf16[512,256]{1,0:T(8,128)(2,1)S(1)}, u32[]{:S(2)}, u32[]{:S(2)}) collective-permute-start(bf16[512,256]{1,0:T(8,128)(2,1)S(1)} %relay.2), channel_id=1, source_target_pairs={{0,64},{32,224},{1,65},{33,225},{2,66},{34,226},{3,67},{35,227},{4... | collective-permute-start | bytes 786440 | tf_op jit(solution)/shard_map/ppermute | solution.py:654
  82.5 3.3 %collective-permute-start.20 = (bf16[512,128]{1,0:T(8,128)(2,1)S(1)}, bf16[512,128]{1,0:T(8,128)(2,1)S(1)}, u32[]{:S(2)}, u32[]{:S(2)}) collective-permute-start(bf16[512,128]{1,0:T(8,128)(2,1)S(1)} %get-tuple-element.106.refs_1_), channel_id=1, source_target_pairs={{0,128},{32,160},{64,192},{96,224},{128,0},{160,32},{192,64},{224,... | collective-permute-start | bytes 393224 | tf_op jit(solution)/shard_map/ppermute | solution.py:58
  85.8 9.5 %attention.4 = (bf16[528,128]{1,0:T(8,128)(2,1)S(1)}, bf16[528,128]{1,0:T(8,128)(2,1)S(1)}) custom-call(s32[8]{0:T(128)S(1)} %stack.187.refs_0_, bf16[512,128]{1,0:T(8,128)(2,1)S(1)} %collective-permute-done.16.refs_1_, bf16[512,128]{1,0:T(8,128)(2,1)S(1)} %collective-permute-done.17.refs_2_, bf16[2048,128]{1,0:T(8,128)(2,1)S(1)} %copy-done.2, ...), custom_call_target="tpu_custom_call" | custom-call | flops 2684354560 | bytes 3145728 | tf_op jit(solution)/shard_map/attention/pallas_call | solution.py:312
  96.4 5.0 %attention.5 = bf16[528,128]{1,0:T(8,128)(2,1)S(1)} custom-call(s32[4]{0:T(128)S(1)} %get-tuple-element.105.refs_0_, bf16[512,128]{1,0:T(8,128)(2,1)S(1)} %collective-permute-done.20.refs_1_, bf16[2048,128]{1,0:T(8,128)(2,1)S(1)} %copy-done.2, bf16[2048,128]{1,0:T(8,128)(2,1)S(1)} %copy-done.3, ...), custom_call_target="tpu_custom_call" | custom-call | flops 1342177280 | bytes 3145728 | tf_op jit(solution)/shard_map/attention/pallas_call | solution.py:312
  101.5 3.9 %collective-permute-done.28.refs_2_.n3 = bf16[128,2560]{1,0:T(8,128)(2,1)S(1)} collective-permute-done((bf16[128,2560]{1,0:T(8,128)(2,1)S(1)}, bf16[128,2560]{1,0:T(8,128)(2,1)S(1)}, u32[]{:S(2)}, u32[]{:S(2)}) %collective-permute-start.28) | collective-permute-done | bytes 655392 | tf_op jit(solution)/shard_map/ppermute | solution.py:154
  105.5 4.1 %collective-permute-start.29 = (bf16[384,2560]{1,0:T(8,128)(2,1)S(1)}, bf16[384,2560]{1,0:T(8,128)(2,1)S(1)}, u32[]{:S(2)}, u32[]{:S(2)}) collective-permute-start(bf16[384,2560]{1,0:T(8,128)(2,1)S(1)} %stack.191), channel_id=1, source_target_pairs={{0,32},{32,0},{1,33},{33,1},{2,34},{34,2},{3,35},{35,3},{4,36},{36... | collective-permute-start | bytes 5898248 | tf_op jit(solution)/shard_map/ppermute | solution.py:62
  109.7 2.6 %collective-permute-start.18 = (bf16[528,128]{1,0:T(8,128)(2,1)S(1)}, bf16[528,128]{1,0:T(8,128)(2,1)S(1)}, u32[]{:S(2)}, u32[]{:S(2)}) collective-permute-start(bf16[528,128]{1,0:T(8,128)(2,1)S(1)} %get-tuple-element.103), channel_id=1, source_target_pairs={{0,32},{32,64},{64,96},{96,128},{128,160},{160,192},{192,224},{224... | collective-permute-start | bytes 405512 | tf_op jit(solution)/shard_map/ppermute | solution.py:58
  112.5 5.4 %collective-permute-start.24 = (bf16[528,128]{1,0:T(8,128)(2,1)S(1)}, bf16[528,128]{1,0:T(8,128)(2,1)S(1)}, u32[]{:S(2)}, u32[]{:S(2)}) collective-permute-start(bf16[528,128]{1,0:T(8,128)(2,1)S(1)} %attention.5), channel_id=1, source_target_pairs={{0,96},{32,128},{64,160},{96,192},{128,224},{160,0},{192,32},{224,... | collective-permute-start | bytes 405512 | tf_op jit(solution)/shard_map/ppermute | solution.py:58
  118.2 3.5 %collective-permute-done.19.refs_2_ = bf16[528,128]{1,0:T(8,128)(2,1)S(1)} collective-permute-done((bf16[528,128]{1,0:T(8,128)(2,1)S(1)}, bf16[528,128]{1,0:T(8,128)(2,1)S(1)}, u32[]{:S(2)}, u32[]{:S(2)}) %collective-permute-start.19) | collective-permute-done | bytes 135200 | tf_op jit(solution)/shard_map/ppermute | solution.py:58
  121.7 5.6 %collective-permute-done.24.refs_3_ = bf16[528,128]{1,0:T(8,128)(2,1)S(1)} collective-permute-done((bf16[528,128]{1,0:T(8,128)(2,1)S(1)}, bf16[528,128]{1,0:T(8,128)(2,1)S(1)}, u32[]{:S(2)}, u32[]{:S(2)}) %collective-permute-start.24) | collective-permute-done | bytes 135200 | tf_op jit(solution)/shard_map/ppermute | solution.py:58
  129.0 2.2 %collective-permute-start.27 = (bf16[128,128]{1,0:T(8,128)(2,1)S(1)}, bf16[128,128]{1,0:T(8,128)(2,1)S(1)}, u32[]{:S(2)}, u32[]{:S(2)}) collective-permute-start(bf16[128,128]{1,0:T(8,128)(2,1)S(1)} %get-tuple-element.142), channel_id=1, source_target_pairs={{0,16},{8,24},{16,0},{24,8},{1,17},{9,25},{17,1},{25,9},{2,18},{10... | collective-permute-start | bytes 98312 | tf_op jit(solution)/shard_map/ppermute | solution.py:673
  132.1 1.3 collective-permute-done.27.t3
  133.4 1.4 out_project.1
  134.9 9.7 %collective-permute-done.30.got_ref = bf16[64,5120]{1,0:T(8,128)(2,1)S(1)} collective-permute-done((bf16[64,5120]{1,0:T(8,128)(2,1)S(1)}, bf16[64,5120]{1,0:T(8,128)(2,1)S(1)}, u32[]{:S(2)}, u32[]{:S(2)}) %collective-permute-start.30) | collective-permute-done | bytes 655392 | tf_op jit(solution)/shard_map/ppermute | solution.py:54
  145.5 4.9 %collective-permute-start.32 = (bf16[512,256]{1,0:T(8,128)(2,1)S(1)}, bf16[512,256]{1,0:T(8,128)(2,1)S(1)}, u32[]{:S(2)}, u32[]{:S(2)}) collective-permute-start(bf16[512,256]{1,0:T(8,128)(2,1)S(1)} %relay.3), channel_id=1, source_target_pairs={{0,128},{32,160},{64,96},{224,192},{1,129},{33,161},{65,97},{225,1... | collective-permute-start | bytes 786440 | tf_op jit(solution)/shard_map/ppermute | solution.py:678
  151.3 4.2 %collective-permute-done.32.second_ref = bf16[512,256]{1,0:T(8,128)(2,1)S(1)} collective-permute-done((bf16[512,256]{1,0:T(8,128)(2,1)S(1)}, bf16[512,256]{1,0:T(8,128)(2,1)S(1)}, u32[]{:S(2)}, u32[]{:S(2)}) %collective-permute-start.32) | collective-permute-done | bytes 262176 | tf_op jit(solution)/shard_map/ppermute | solution.py:678
  156.2 6.8 %collective-permute-done.33.got_ref = bf16[16,5120]{1,0:T(8,128)(2,1)S(1)} collective-permute-done((bf16[16,5120]{1,0:T(8,128)(2,1)S(1)}, bf16[16,5120]{1,0:T(8,128)(2,1)S(1)}, u32[]{:S(2)}, u32[]{:S(2)}) %collective-permute-start.33) | collective-permute-done | bytes 163872 | tf_op jit(solution)/shard_map/ppermute | solution.py:54
  163.9 1.3 collective-permute-start.36
  165.9 1.7 insert_rows.1
  167.6 5.8 %collective-permute-done.36 = bf16[16,5120]{1,0:T(8,128)(2,1)S(1)} collective-permute-done((bf16[16,5120]{1,0:T(8,128)(2,1)S(1)}, bf16[16,5120]{1,0:T(8,128)(2,1)S(1)}, u32[]{:S(2)}, u32[]{:S(2)}) %collective-permute-start.36) | collective-permute-done | bytes 163872 | tf_op jit(solution)/shard_map/ppermute | solution.py:689
  174.1 1.3 collective-permute-start.38
  (84 shorter events, 16.0 us)
Async XLA Ops:
  0.6 1.4 copy-start
  3.2 0.9 copy-start.4
  4.5 0.7 copy-start.5
  5.2 5.9 %collective-permute-start = (bf16[16,5120]{1,0:T(8,128)(2,1)S(1)}, bf16[16,5120]{1,0:T(8,128)(2,1)}, u32[]{:S(2)}, u32[]{:S(2)}) collective-permute-start(bf16[16,5120]{1,0:T(8,128)(2,1)S(1)} %get-tuple-element.71.refs_0_), channel_id=1, source_target_pairs={{0,4},{4,0},{1,5},{5,1},{2,6},{6,2},{3,7},{7,3},{8,12},{12,8},{9,1... | collective-permute-start | bytes 491528 | tf_op jit(solution)/shard_map/ppermute | solution.py:39
  9.7 22.5 %copy-start.2 = (bf16[2048,128]{1,0:T(8,128)(2,1)S(1)}, bf16[2048,128]{1,0:T(8,128)(2,1)}, u32[]{:S(2)}) copy-start(bf16[2048,128]{1,0:T(8,128)(2,1)} %k_ref.1) | copy-start | bytes 1572868
  9.7 22.5 %copy-start.3 = (bf16[2048,128]{1,0:T(8,128)(2,1)S(1)}, bf16[2048,128]{1,0:T(8,128)(2,1)}, u32[]{:S(2)}) copy-start(bf16[2048,128]{1,0:T(8,128)(2,1)} %v_ref.1) | copy-start | bytes 1572868
  12.1 6.0 %collective-permute-start.1 = (bf16[32,2560]{1,0:T(8,128)(2,1)S(1)}, bf16[32,2560]{1,0:T(8,128)(2,1)S(1)}, u32[]{:S(2)}, u32[]{:S(2)}) collective-permute-start(bf16[32,2560]{1,0:T(8,128)(2,1)S(1)} %get-tuple-element.85.refs_0_), channel_id=1, source_target_pairs={{0,8},{8,16},{16,24},{24,0},{1,9},{9,17},{17,25},{25,1},{2,10},{10... | collective-permute-start | bytes 491528 | tf_op jit(solution)/shard_map/ppermute | solution.py:158
  13.8 4.2 %collective-permute-start.2 = (bf16[32,2560]{1,0:T(8,128)(2,1)S(1)}, bf16[32,2560]{1,0:T(8,128)(2,1)S(1)}, u32[]{:S(2)}, u32[]{:S(2)}) collective-permute-start(bf16[32,2560]{1,0:T(8,128)(2,1)S(1)} %get-tuple-element.85.refs_0_), channel_id=1, source_target_pairs={{0,24},{8,0},{16,8},{24,16},{1,25},{9,1},{17,9},{25,17},{2,26},{10... | collective-permute-start | bytes 491528 | tf_op jit(solution)/shard_map/ppermute | solution.py:159
  15.2 5.8 %collective-permute-start.4 = (bf16[32,2560]{1,0:T(8,128)(2,1)S(1)}, bf16[32,2560]{1,0:T(8,128)(2,1)S(1)}, u32[]{:S(2)}, u32[]{:S(2)}) collective-permute-start(bf16[32,2560]{1,0:T(8,128)(2,1)S(1)} %get-tuple-element.86.refs_4_), channel_id=1, source_target_pairs={{0,1},{1,2},{2,3},{3,0},{4,5},{5,6},{6,7},{7,4},{8,9},{9,10},{10,1... | collective-permute-start | bytes 491528 | tf_op jit(solution)/shard_map/ppermute | solution.py:158
  16.6 4.4 %collective-permute-start.5 = (bf16[32,2560]{1,0:T(8,128)(2,1)S(1)}, bf16[32,2560]{1,0:T(8,128)(2,1)S(1)}, u32[]{:S(2)}, u32[]{:S(2)}) collective-permute-start(bf16[32,2560]{1,0:T(8,128)(2,1)S(1)} %get-tuple-element.86.refs_4_), channel_id=1, source_target_pairs={{0,3},{1,0},{2,1},{3,2},{4,7},{5,4},{6,5},{7,6},{8,11},{9,8},{10,9... | collective-permute-start | bytes 491528 | tf_op jit(solution)/shard_map/ppermute | solution.py:159
  18.1 5.6 %collective-permute-start.3 = (bf16[32,2560]{1,0:T(8,128)(2,1)S(1)}, bf16[32,2560]{1,0:T(8,128)(2,1)S(1)}, u32[]{:S(2)}, u32[]{:S(2)}) collective-permute-start(bf16[32,2560]{1,0:T(8,128)(2,1)S(1)} %pick.5), channel_id=1, source_target_pairs={{0,8},{8,16},{16,24},{24,0},{32,56},{40,32},{48,40},{56,48},{1,9},... | collective-permute-start | bytes 491528 | tf_op jit(solution)/shard_map/ppermute | solution.py:154
  21.0 4.8 %collective-permute-start.6 = (bf16[32,2560]{1,0:T(8,128)(2,1)S(1)}, bf16[32,2560]{1,0:T(8,128)(2,1)S(1)}, u32[]{:S(2)}, u32[]{:S(2)}) collective-permute-start(bf16[32,2560]{1,0:T(8,128)(2,1)S(1)} %pick.6), channel_id=1, source_target_pairs={{0,1},{1,2},{2,3},{3,0},{32,35},{33,32},{34,33},{35,34},{4,5},{5,6... | collective-permute-start | bytes 491528 | tf_op jit(solution)/shard_map/ppermute | solution.py:154
  26.0 13.8 %collective-permute-start.7 = (bf16[128,2560]{1,0:T(8,128)(2,1)S(1)}, bf16[128,2560]{1,0:T(8,128)(2,1)S(1)}, u32[]{:S(2)}, u32[]{:S(2)}) collective-permute-start(bf16[128,2560]{1,0:T(8,128)(2,1)S(1)} %get-tuple-element.89.refs_1_), channel_id=1, source_target_pairs={{0,1},{1,2},{2,3},{3,0},{4,5},{5,6},{6,7},{7,4},{8,9},{9,10},{10,1... | collective-permute-start | bytes 1966088 | tf_op jit(solution)/shard_map/ppermute | solution.py:158
  27.1 12.7 %collective-permute-start.9 = (bf16[128,2560]{1,0:T(8,128)(2,1)S(1)}, bf16[128,2560]{1,0:T(8,128)(2,1)S(1)}, u32[]{:S(2)}, u32[]{:S(2)}) collective-permute-start(bf16[128,2560]{1,0:T(8,128)(2,1)S(1)} %get-tuple-element.89.refs_1_), channel_id=1, source_target_pairs={{0,3},{1,0},{2,1},{3,2},{4,7},{5,4},{6,5},{7,6},{8,11},{9,8},{10,9... | collective-permute-start | bytes 1966088 | tf_op jit(solution)/shard_map/ppermute | solution.py:159
  29.5 13.1 %collective-permute-start.8 = (bf16[128,2560]{1,0:T(8,128)(2,1)S(1)}, bf16[128,2560]{1,0:T(8,128)(2,1)S(1)}, u32[]{:S(2)}, u32[]{:S(2)}) collective-permute-start(bf16[128,2560]{1,0:T(8,128)(2,1)S(1)} %get-tuple-element.90.refs_2_), channel_id=1, source_target_pairs={{0,8},{8,16},{16,24},{24,0},{1,9},{9,17},{17,25},{25,1},{2,10},{10... | collective-permute-start | bytes 1966088 | tf_op jit(solution)/shard_map/ppermute | solution.py:158
  29.5 13.1 %collective-permute-start.10 = (bf16[128,2560]{1,0:T(8,128)(2,1)S(1)}, bf16[128,2560]{1,0:T(8,128)(2,1)S(1)}, u32[]{:S(2)}, u32[]{:S(2)}) collective-permute-start(bf16[128,2560]{1,0:T(8,128)(2,1)S(1)} %get-tuple-element.90.refs_2_), channel_id=1, source_target_pairs={{0,24},{8,0},{16,8},{24,16},{1,25},{9,1},{17,9},{25,17},{2,26},{10... | collective-permute-start | bytes 1966088 | tf_op jit(solution)/shard_map/ppermute | solution.py:159
  32.4 12.0 %copy-start.1 = (bf16[3,5120,128]{2,1,0:T(8,128)(2,1)S(1)}, bf16[3,5120,128]{2,1,0:T(8,128)(2,1)}, u32[]{:S(2)}) copy-start(bf16[3,5120,128]{2,1,0:T(8,128)(2,1)} %refs_3_.6) | copy-start | bytes 11796484
  32.4 16.7 %collective-permute-start.13 = (bf16[2048,256]{1,0:T(8,128)(2,1)S(1)}, bf16[2048,256]{1,0:T(8,128)(2,1)S(1)}, u32[]{:S(2)}, u32[]{:S(2)}) collective-permute-start(bf16[2048,256]{1,0:T(8,128)(2,1)S(1)} %beside.1), channel_id=1, source_target_pairs={{0,32},{32,0},{1,33},{33,1},{2,34},{34,2},{3,35},{35,3},{4,36},{36... | collective-permute-start | bytes 3145736 | tf_op jit(solution)/shard_map/ppermute | solution.py:62
  39.8 11.3 %collective-permute-start.11 = (bf16[128,2560]{1,0:T(8,128)(2,1)S(1)}, bf16[128,2560]{1,0:T(8,128)(2,1)S(1)}, u32[]{:S(2)}, u32[]{:S(2)}) collective-permute-start(bf16[128,2560]{1,0:T(8,128)(2,1)S(1)} %pick.7), channel_id=1, source_target_pairs={{0,1},{1,2},{2,3},{3,0},{32,35},{33,32},{34,33},{35,34},{4,5},{5,6... | collective-permute-start | bytes 1966088 | tf_op jit(solution)/shard_map/ppermute | solution.py:154
  42.6 11.1 %collective-permute-start.12 = (bf16[128,2560]{1,0:T(8,128)(2,1)S(1)}, bf16[128,2560]{1,0:T(8,128)(2,1)S(1)}, u32[]{:S(2)}, u32[]{:S(2)}) collective-permute-start(bf16[128,2560]{1,0:T(8,128)(2,1)S(1)} %pick.8), channel_id=1, source_target_pairs={{0,8},{8,16},{16,24},{24,0},{32,56},{40,32},{48,40},{56,48},{1,9},... | collective-permute-start | bytes 1966088 | tf_op jit(solution)/shard_map/ppermute | solution.py:154
  55.6 9.0 %collective-permute-start.14 = (bf16[512,256]{1,0:T(8,128)(2,1)S(1)}, bf16[512,256]{1,0:T(8,128)(2,1)S(1)}, u32[]{:S(2)}, u32[]{:S(2)}) collective-permute-start(bf16[512,256]{1,0:T(8,128)(2,1)S(1)} %get-tuple-element.99.refs_5_.refs_6_.own_ref.got_ref), channel_id=1, source_target_pairs={{0,32},{32,0},{1,33},{33,1},{2,34},{34,2},{3,35},{35,3},{4,36},{36... | collective-permute-start | bytes 786440 | tf_op jit(solution)/shard_map/ppermute | solution.py:62
  69.7 25.6 %collective-permute-start.21 = (bf16[128,2560]{1,0:T(8,128)(2,1)S(1)}, bf16[128,2560]{1,0:T(8,128)(2,1)S(1)}, u32[]{:S(2)}, u32[]{:S(2)}) collective-permute-start(bf16[128,2560]{1,0:T(8,128)(2,1)S(1)} %get-tuple-element.107.n0), channel_id=1, source_target_pairs={{0,8},{8,0},{16,24},{24,16},{1,9},{9,1},{17,25},{25,17},{2,10},{10... | collective-permute-start | bytes 1966088 | tf_op jit(solution)/shard_map/ppermute | solution.py:39
  69.8 25.5 %collective-permute-start.22 = (bf16[128,2560]{1,0:T(8,128)(2,1)S(1)}, bf16[128,2560]{1,0:T(8,128)(2,1)S(1)}, u32[]{:S(2)}, u32[]{:S(2)}) collective-permute-start(bf16[128,2560]{1,0:T(8,128)(2,1)S(1)} %get-tuple-element.107.n0), channel_id=1, source_target_pairs={{0,24},{8,16},{16,8},{24,0},{1,25},{9,17},{17,9},{25,1},{2,26},{10... | collective-permute-start | bytes 1966088 | tf_op jit(solution)/shard_map/ppermute | solution.py:39
  71.6 10.9 %collective-permute-start.16 = (bf16[512,128]{1,0:T(8,128)(2,1)S(1)}, bf16[512,128]{1,0:T(8,128)(2,1)S(1)}, u32[]{:S(2)}, u32[]{:S(2)}) collective-permute-start(bf16[512,128]{1,0:T(8,128)(2,1)S(1)} %get-tuple-element.106.refs_1_), channel_id=1, source_target_pairs={{0,192},{32,224},{64,0},{96,32},{128,64},{160,96},{192,128},{224,1... | collective-permute-start | bytes 393224 | tf_op jit(solution)/shard_map/ppermute | solution.py:58
  76.9 8.9 %collective-permute-start.17 = (bf16[512,128]{1,0:T(8,128)(2,1)S(1)}, bf16[512,128]{1,0:T(8,128)(2,1)S(1)}, u32[]{:S(2)}, u32[]{:S(2)}) collective-permute-start(bf16[512,128]{1,0:T(8,128)(2,1)S(1)} %get-tuple-element.106.refs_1_), channel_id=1, source_target_pairs={{0,64},{32,96},{64,128},{96,160},{128,192},{160,224},{192,0},{224,... | collective-permute-start | bytes 393224 | tf_op jit(solution)/shard_map/ppermute | solution.py:58
  77.0 18.3 %collective-permute-start.23 = (bf16[512,256]{1,0:T(8,128)(2,1)S(1)}, bf16[512,256]{1,0:T(8,128)(2,1)S(1)}, u32[]{:S(2)}, u32[]{:S(2)}) collective-permute-start(bf16[512,256]{1,0:T(8,128)(2,1)S(1)} %relay.2), channel_id=1, source_target_pairs={{0,64},{32,224},{1,65},{33,225},{2,66},{34,226},{3,67},{35,227},{4... | collective-permute-start | bytes 786440 | tf_op jit(solution)/shard_map/ppermute | solution.py:654
  82.5 12.8 %collective-permute-start.20 = (bf16[512,128]{1,0:T(8,128)(2,1)S(1)}, bf16[512,128]{1,0:T(8,128)(2,1)S(1)}, u32[]{:S(2)}, u32[]{:S(2)}) collective-permute-start(bf16[512,128]{1,0:T(8,128)(2,1)S(1)} %get-tuple-element.106.refs_1_), channel_id=1, source_target_pairs={{0,128},{32,160},{64,192},{96,224},{128,0},{160,32},{192,64},{224,... | collective-permute-start | bytes 393224 | tf_op jit(solution)/shard_map/ppermute | solution.py:58
  95.4 10.0 %collective-permute-start.28 = (bf16[128,2560]{1,0:T(8,128)(2,1)S(1)}, bf16[128,2560]{1,0:T(8,128)(2,1)S(1)}, u32[]{:S(2)}, u32[]{:S(2)}) collective-permute-start(bf16[128,2560]{1,0:T(8,128)(2,1)S(1)} %pick.9), channel_id=1, source_target_pairs={{0,24},{8,16},{16,8},{24,0},{32,40},{40,32},{48,56},{56,48},{1,25}... | collective-permute-start | bytes 1966088 | tf_op jit(solution)/shard_map/ppermute | solution.py:154
  105.5 27.8 %collective-permute-start.29 = (bf16[384,2560]{1,0:T(8,128)(2,1)S(1)}, bf16[384,2560]{1,0:T(8,128)(2,1)S(1)}, u32[]{:S(2)}, u32[]{:S(2)}) collective-permute-start(bf16[384,2560]{1,0:T(8,128)(2,1)S(1)} %stack.191), channel_id=1, source_target_pairs={{0,32},{32,0},{1,33},{33,1},{2,34},{34,2},{3,35},{35,3},{4,36},{36... | collective-permute-start | bytes 5898248 | tf_op jit(solution)/shard_map/ppermute | solution.py:62
  109.6 8.5 %collective-permute-start.15 = (bf16[528,128]{1,0:T(8,128)(2,1)S(1)}, bf16[528,128]{1,0:T(8,128)(2,1)S(1)}, u32[]{:S(2)}, u32[]{:S(2)}) collective-permute-start(bf16[528,128]{1,0:T(8,128)(2,1)S(1)} %attention.3), channel_id=1, source_target_pairs={{0,224},{32,0},{64,32},{96,64},{128,96},{160,128},{192,160},{224,1... | collective-permute-start | bytes 405512 | tf_op jit(solution)/shard_map/ppermute | solution.py:58
  109.7 8.5 %collective-permute-start.18 = (bf16[528,128]{1,0:T(8,128)(2,1)S(1)}, bf16[528,128]{1,0:T(8,128)(2,1)S(1)}, u32[]{:S(2)}, u32[]{:S(2)}) collective-permute-start(bf16[528,128]{1,0:T(8,128)(2,1)S(1)} %get-tuple-element.103), channel_id=1, source_target_pairs={{0,32},{32,64},{64,96},{96,128},{128,160},{160,192},{192,224},{224... | collective-permute-start | bytes 405512 | tf_op jit(solution)/shard_map/ppermute | solution.py:58
  112.3 9.4 %collective-permute-start.19 = (bf16[528,128]{1,0:T(8,128)(2,1)S(1)}, bf16[528,128]{1,0:T(8,128)(2,1)S(1)}, u32[]{:S(2)}, u32[]{:S(2)}) collective-permute-start(bf16[528,128]{1,0:T(8,128)(2,1)S(1)} %get-tuple-element.104), channel_id=1, source_target_pairs={{0,160},{32,192},{64,224},{96,0},{128,32},{160,64},{192,96},{224,1... | collective-permute-start | bytes 405512 | tf_op jit(solution)/shard_map/ppermute | solution.py:58
  112.5 14.8 %collective-permute-start.24 = (bf16[528,128]{1,0:T(8,128)(2,1)S(1)}, bf16[528,128]{1,0:T(8,128)(2,1)S(1)}, u32[]{:S(2)}, u32[]{:S(2)}) collective-permute-start(bf16[528,128]{1,0:T(8,128)(2,1)S(1)} %attention.5), channel_id=1, source_target_pairs={{0,96},{32,128},{64,160},{96,192},{128,224},{160,0},{192,32},{224,... | collective-permute-start | bytes 405512 | tf_op jit(solution)/shard_map/ppermute | solution.py:58
  127.9 3.3 %collective-permute-start.25 = (bf16[128,128]{1,0:T(8,128)(2,1)S(1)}, bf16[128,128]{1,0:T(8,128)(2,1)S(1)}, u32[]{:S(2)}, u32[]{:S(2)}) collective-permute-start(bf16[128,128]{1,0:T(8,128)(2,1)S(1)} %get-tuple-element.144), channel_id=1, source_target_pairs={{0,8},{8,0},{16,24},{24,16},{1,9},{9,1},{17,25},{25,17},{2,10},{10... | collective-permute-start | bytes 98312 | tf_op jit(solution)/shard_map/ppermute | solution.py:39
  128.0 4.1 %collective-permute-start.26 = (bf16[128,128]{1,0:T(8,128)(2,1)S(1)}, bf16[128,128]{1,0:T(8,128)(2,1)S(1)}, u32[]{:S(2)}, u32[]{:S(2)}) collective-permute-start(bf16[128,128]{1,0:T(8,128)(2,1)S(1)} %get-tuple-element.143), channel_id=1, source_target_pairs={{0,24},{8,16},{16,8},{24,0},{1,25},{9,17},{17,9},{25,1},{2,26},{10... | collective-permute-start | bytes 98312 | tf_op jit(solution)/shard_map/ppermute | solution.py:39
  129.0 4.4 %collective-permute-start.27 = (bf16[128,128]{1,0:T(8,128)(2,1)S(1)}, bf16[128,128]{1,0:T(8,128)(2,1)S(1)}, u32[]{:S(2)}, u32[]{:S(2)}) collective-permute-start(bf16[128,128]{1,0:T(8,128)(2,1)S(1)} %get-tuple-element.142), channel_id=1, source_target_pairs={{0,16},{8,24},{16,0},{24,8},{1,17},{9,25},{17,1},{25,9},{2,18},{10... | collective-permute-start | bytes 98312 | tf_op jit(solution)/shard_map/ppermute | solution.py:673
  134.8 15.6 %copy-start.6 = (bf16[32,5120]{1,0:T(8,128)(2,1)S(1)}, bf16[32,5120]{1,0:T(8,128)(2,1)}, u32[]{:S(2)}) copy-start(bf16[32,5120]{1,0:T(8,128)(2,1)} %copy-done.5) | copy-start | bytes 983044
  134.8 9.8 %collective-permute-start.30 = (bf16[64,5120]{1,0:T(8,128)(2,1)S(1)}, bf16[64,5120]{1,0:T(8,128)(2,1)S(1)}, u32[]{:S(2)}, u32[]{:S(2)}) collective-permute-start(bf16[64,5120]{1,0:T(8,128)(2,1)S(1)} %get-tuple-element.116), channel_id=1, source_target_pairs={{0,4},{1,5},{2,6},{3,7},{4,0},{5,1},{6,2},{7,3},{8,12},{9,13},{10,... | collective-permute-start | bytes 1966088 | tf_op jit(solution)/shard_map/ppermute | solution.py:54
  144.8 10.7 %collective-permute-start.31 = (bf16[32,5120]{1,0:T(8,128)(2,1)S(1)}, bf16[32,5120]{1,0:T(8,128)(2,1)S(1)}, u32[]{:S(2)}, u32[]{:S(2)}) collective-permute-start(bf16[32,5120]{1,0:T(8,128)(2,1)S(1)} %get-tuple-element.118), channel_id=1, source_target_pairs={{0,1},{1,0},{2,3},{3,2},{4,5},{5,4},{6,7},{7,6},{8,9},{9,8},{10,11... | collective-permute-start | bytes 983048 | tf_op jit(solution)/shard_map/ppermute | solution.py:54
  145.5 10.0 %collective-permute-start.32 = (bf16[512,256]{1,0:T(8,128)(2,1)S(1)}, bf16[512,256]{1,0:T(8,128)(2,1)S(1)}, u32[]{:S(2)}, u32[]{:S(2)}) collective-permute-start(bf16[512,256]{1,0:T(8,128)(2,1)S(1)} %relay.3), channel_id=1, source_target_pairs={{0,128},{32,160},{64,96},{224,192},{1,129},{33,161},{65,97},{225,1... | collective-permute-start | bytes 786440 | tf_op jit(solution)/shard_map/ppermute | solution.py:678
  150.4 12.7 %collective-permute-start.34 = (bf16[32,5120]{1,0:T(8,128)(2,1)S(1)}, bf16[32,5120]{1,0:T(8,128)(2,1)S(1)}, u32[]{:S(2)}, u32[]{:S(2)}) collective-permute-start(bf16[32,5120]{1,0:T(8,128)(2,1)S(1)} %copy-done.6), channel_id=1, source_target_pairs={{0,224},{32,0},{64,32},{96,64},{128,96},{160,128},{192,160},{224,1... | collective-permute-start | bytes 983048 | tf_op jit(solution)/shard_map/ppermute | solution.py:58
  155.5 7.5 %collective-permute-start.33 = (bf16[16,5120]{1,0:T(8,128)(2,1)S(1)}, bf16[16,5120]{1,0:T(8,128)(2,1)S(1)}, u32[]{:S(2)}, u32[]{:S(2)}) collective-permute-start(bf16[16,5120]{1,0:T(8,128)(2,1)S(1)} %get-tuple-element.123), channel_id=1, source_target_pairs={{0,3},{1,2},{2,1},{3,0},{4,7},{5,6},{6,5},{7,4},{8,11},{9,10},{10,... | collective-permute-start | bytes 491528 | tf_op jit(solution)/shard_map/ppermute | solution.py:54
  163.2 4.4 %collective-permute-start.35 = (bf16[16,5120]{1,0:T(8,128)(2,1)S(1)}, bf16[16,5120]{1,0:T(8,128)(2,1)S(1)}, u32[]{:S(2)}, u32[]{:S(2)}) collective-permute-start(bf16[16,5120]{1,0:T(8,128)(2,1)S(1)} %finish.1), channel_id=1, source_target_pairs={{224,96},{225,97},{226,98},{227,99},{228,100},{229,101},{230,102},... | collective-permute-start | bytes 491528 | tf_op jit(solution)/shard_map/ppermute | solution.py:689
  163.9 9.5 %collective-permute-start.36 = (bf16[16,5120]{1,0:T(8,128)(2,1)S(1)}, bf16[16,5120]{1,0:T(8,128)(2,1)S(1)}, u32[]{:S(2)}, u32[]{:S(2)}) collective-permute-start(bf16[16,5120]{1,0:T(8,128)(2,1)S(1)} %finish.1), channel_id=1, source_target_pairs={{224,32},{225,33},{226,34},{227,35},{228,36},{229,37},{230,38},{23... | collective-permute-start | bytes 491528 | tf_op jit(solution)/shard_map/ppermute | solution.py:689
  165.2 8.2 %collective-permute-start.37 = (bf16[16,5120]{1,0:T(8,128)(2,1)S(1)}, bf16[16,5120]{1,0:T(8,128)(2,1)S(1)}, u32[]{:S(2)}, u32[]{:S(2)}) collective-permute-start(bf16[16,5120]{1,0:T(8,128)(2,1)S(1)} %finish.1), channel_id=1, source_target_pairs={{224,160},{225,161},{226,162},{227,163},{228,164},{229,165},{230,1... | collective-permute-start | bytes 491528 | tf_op jit(solution)/shard_map/ppermute | solution.py:689
  174.1 2.3 %collective-permute-start.38 = (bf16[16,5120]{1,0:T(8,128)(2,1)S(1)}, bf16[16,5120]{1,0:T(8,128)(2,1)S(1)}, u32[]{:S(2)}, u32[]{:S(2)}) collective-permute-start(bf16[16,5120]{1,0:T(8,128)(2,1)S(1)} %get-tuple-element.140), channel_id=1, source_target_pairs={{32,0},{33,1},{34,2},{35,3},{36,4},{37,5},{38,6},{39,7},{40,8},{41... | collective-permute-start | bytes 491528 | tf_op jit(solution)/shard_map/ppermute | solution.py:695
